TPU v7x, 32 devices: a whole 2x2x4 slice. The times are simulated.
32 devices in a mesh: dp: 2 (over x), expert: 16 (over z, y, core).
Axes of the slice: x: 2, y: 2, z: 4, core: 2. Of those that a mesh axis runs over, the one named last changes fastest.
Arguments:
- tokens: bfloat16 [2048, 4096], P('expert', 'dp'), may hold values from -6 to 6
- expert_ids: int32 [2048, 8], P('expert'), may hold values from 0 to 15, all different within a row; in each aligned block of 128 rows (0 to 127, 128 to 255, ...) at most 96 rows name the same one
- gates: float32 [2048, 8], P('expert'), may hold values from 0.1 to 0.6
- cotangent: bfloat16 [2048, 4096], P('expert', 'dp'), may hold values from -0.59765625 to 0.59765625
- partner: int32 [16], replicated, may hold values from -1 to 15, as said below
- w_gate: bfloat16 [16, 4096, 1024], P('expert', 'dp'), may hold values from -0.09375 to 0.09375
- w_up: bfloat16 [16, 4096, 1024], P('expert', 'dp'), may hold values from -0.09375 to 0.09375
- w_down: bfloat16 [16, 1024, 4096], P('expert', None, 'dp'), may hold values from -0.1875 to 0.1875
Outputs:
- mixed: bfloat16 [2048, 4096], P('expert', 'dp')
- grad_tokens: bfloat16 [2048, 4096], P('expert', 'dp')
- grad_gates: float32 [2048, 8], P('expert')
- grad_gate_w: bfloat16 [16, 4096, 1024], P('expert', 'dp')
- grad_up_w: bfloat16 [16, 4096, 1024], P('expert', 'dp')
- grad_down_w: bfloat16 [16, 1024, 4096], P('expert', None, 'dp')
Inputs may be any that keep to these rules, and one draw needn't show every extreme that they name: `expert_ids`: each row names 8 different experts. In each aligned block of 128 rows no expert is named more than 64 + 32 times, and in some block some expert is named exactly that many times. Exactly 8 entries are -1. The others name distinct experts, and for each such expert e, partner[e] is -1.
All inputs are finite; a program needn't handle non-finite values.
Results may differ from a plain program's by a relative error of at most 0.023.
Values may be sent and summed in bfloat16 or wider, within the bound.
A program may use at most 192 MiB of HBM per device.

v0:
```python
import jax
import jax.numpy as jnp
from jax import lax
from jax.sharding import PartitionSpec as P


def matmul(left, right):
    return jnp.dot(left, right, preferred_element_type=jnp.float32)


def matmul_bt(left, right):
    return lax.dot_general(
        left, right, (((1,), (1,)), ((), ())), preferred_element_type=jnp.float32
    )


def matmul_at(left, right):
    return lax.dot_general(
        left, right, (((0,), (0,)), ((), ())), preferred_element_type=jnp.float32
    )


def swiglu_parts(gate_pre, up_pre, dhid):
    sig = jax.nn.sigmoid(gate_pre)
    act = gate_pre * sig
    hid = (act * up_pre).astype(jnp.bfloat16)
    dup = (dhid * act).astype(jnp.bfloat16)
    dgate = (dhid * up_pre * sig * (1.0 + gate_pre * (1.0 - sig))).astype(jnp.bfloat16)
    return (hid, dgate, dup)


def fill_slots(index, values, count, filler):
    return jnp.full((count + 1,), filler, values.dtype).at[index].set(values)[:count]


def local(tokens, expert_ids, gates, cotangent, partner, w_gate, w_up, w_down):
    n_exp = lax.axis_size("expert")
    rows, width = tokens.shape
    top = expert_ids.shape[1]
    cap = rows * top // n_exp
    spill = cap // 2
    home_total = n_exp * cap
    spill_total = n_exp * spill
    flat_ids = expert_ids.reshape(-1)
    labels = jnp.arange(n_exp, dtype=jnp.int32)
    onehot = (flat_ids[:, None] == labels[None, :]).astype(jnp.int32)
    rank = jnp.sum((jnp.cumsum(onehot, axis=0) - 1) * onehot, axis=1)
    matched = (partner[:, None] == labels[None, :]).astype(jnp.int32)
    hosted = jnp.sum(matched, axis=0)
    host_dev = jnp.sum(matched * labels[:, None], axis=0)
    pair_hosted = jnp.sum(onehot * hosted[None, :], axis=1)
    pair_host = jnp.sum(onehot * host_dev[None, :], axis=1)
    at_home = rank < cap
    spilled = jnp.logical_and(rank >= cap, pair_hosted > 0)
    home_index = jnp.where(at_home, flat_ids * cap + rank, home_total)
    spill_index = jnp.where(spilled, pair_host * spill + rank - cap, spill_total)
    pair_owner = jnp.arange(rows * top, dtype=jnp.int32) // top
    flat_gates = gates.reshape(-1)
    home_source = fill_slots(home_index, pair_owner, home_total, rows)
    spill_source = fill_slots(spill_index, pair_owner, spill_total, rows)
    home_weight = fill_slots(home_index, flat_gates, home_total, 0.0)
    spill_weight = fill_slots(spill_index, flat_gates, spill_total, 0.0)
    tok_pad = jnp.concatenate([tokens, jnp.zeros((1, width), jnp.bfloat16)], axis=0)
    cot_pad = jnp.concatenate([cotangent, jnp.zeros((1, width), jnp.bfloat16)], axis=0)

    def gather_rows(source, weight):
        x_rows = tok_pad[source]
        d_rows = (weight[:, None] * cot_pad[source].astype(jnp.float32)).astype(jnp.bfloat16)
        return (x_rows, d_rows)

    home_x, home_d = gather_rows(home_source, home_weight)
    spill_x, spill_d = gather_rows(spill_source, spill_weight)
    arrived = (
        lax.all_to_all(
            home_x.reshape(n_exp, cap, width), "expert", split_axis=0, concat_axis=0, tiled=True
        ),
        lax.all_to_all(
            home_d.reshape(n_exp, cap, width), "expert", split_axis=0, concat_axis=0, tiled=True
        ),
        lax.all_to_all(
            spill_x.reshape(n_exp, spill, width), "expert", split_axis=0, concat_axis=0, tiled=True
        ),
        lax.all_to_all(
            spill_d.reshape(n_exp, spill, width), "expert", split_axis=0, concat_axis=0, tiled=True
        ),
    )
    home_x = arrived[0].reshape(home_total, width)
    home_d = arrived[1].reshape(home_total, width)
    spill_x = arrived[2].reshape(spill_total, width)
    spill_d = arrived[3].reshape(spill_total, width)
    own_gate = w_gate[0]
    own_up = w_up[0]
    own_down = w_down[0]
    hidden = own_gate.shape[1]
    part_rows = width // n_exp
    part_hidden = hidden // n_exp
    spread = (
        lax.all_to_all(
            own_gate.reshape(n_exp, part_rows, hidden),
            "expert",
            split_axis=0,
            concat_axis=0,
            tiled=True,
        ),
        lax.all_to_all(
            own_up.reshape(n_exp, part_rows, hidden),
            "expert",
            split_axis=0,
            concat_axis=0,
            tiled=True,
        ),
        lax.all_to_all(
            own_down.reshape(n_exp, part_hidden, width),
            "expert",
            split_axis=0,
            concat_axis=0,
            tiled=True,
        ),
    )
    wanted = jnp.maximum(partner, 0)
    keep = (partner >= 0).astype(jnp.bfloat16)[:, None, None]
    copies = (
        lax.all_to_all(spread[0][wanted] * keep, "expert", split_axis=0, concat_axis=0, tiled=True),
        lax.all_to_all(spread[1][wanted] * keep, "expert", split_axis=0, concat_axis=0, tiled=True),
        lax.all_to_all(spread[2][wanted] * keep, "expert", split_axis=0, concat_axis=0, tiled=True),
    )
    copy_gate = copies[0].reshape(width, hidden)
    copy_up = copies[1].reshape(width, hidden)
    copy_down = copies[2].reshape(hidden, width)
    summed = (
        lax.psum_scatter(
            matmul(home_x, own_gate).astype(jnp.bfloat16), "dp", scatter_dimension=1, tiled=True
        ).astype(jnp.float32),
        lax.psum_scatter(
            matmul(home_x, own_up).astype(jnp.bfloat16), "dp", scatter_dimension=1, tiled=True
        ).astype(jnp.float32),
        lax.psum_scatter(
            matmul_bt(home_d, own_down).astype(jnp.bfloat16), "dp", scatter_dimension=1, tiled=True
        ).astype(jnp.float32),
        lax.psum_scatter(
            matmul(spill_x, copy_gate).astype(jnp.bfloat16), "dp", scatter_dimension=1, tiled=True
        ).astype(jnp.float32),
        lax.psum_scatter(
            matmul(spill_x, copy_up).astype(jnp.bfloat16), "dp", scatter_dimension=1, tiled=True
        ).astype(jnp.float32),
        lax.psum_scatter(
            matmul_bt(spill_d, copy_down).astype(jnp.bfloat16),
            "dp",
            scatter_dimension=1,
            tiled=True,
        ).astype(jnp.float32),
    )
    home_parts = swiglu_parts(summed[0], summed[1], summed[2])
    spill_parts = swiglu_parts(summed[3], summed[4], summed[5])
    gathered = (
        lax.all_gather(home_parts[0], "dp", axis=1, tiled=True),
        lax.all_gather(home_parts[1], "dp", axis=1, tiled=True),
        lax.all_gather(home_parts[2], "dp", axis=1, tiled=True),
        lax.all_gather(spill_parts[0], "dp", axis=1, tiled=True),
        lax.all_gather(spill_parts[1], "dp", axis=1, tiled=True),
        lax.all_gather(spill_parts[2], "dp", axis=1, tiled=True),
    )
    home_hid, home_dgate, home_dup, spill_hid, spill_dgate, spill_dup = gathered
    home_out = matmul(home_hid, own_down).astype(jnp.bfloat16)
    spill_out = matmul(spill_hid, copy_down).astype(jnp.bfloat16)
    home_dx = (matmul_bt(home_dgate, own_gate) + matmul_bt(home_dup, own_up)).astype(jnp.bfloat16)
    spill_dx = (matmul_bt(spill_dgate, copy_gate) + matmul_bt(spill_dup, copy_up)).astype(
        jnp.bfloat16
    )
    copy_grad_gate = matmul_at(spill_x, spill_dgate).astype(jnp.bfloat16)
    copy_grad_up = matmul_at(spill_x, spill_dup).astype(jnp.bfloat16)
    copy_grad_down = matmul_at(spill_hid, spill_d).astype(jnp.bfloat16)
    spread_grads = (
        lax.all_to_all(
            copy_grad_gate.reshape(n_exp, part_rows, hidden),
            "expert",
            split_axis=0,
            concat_axis=0,
            tiled=True,
        ),
        lax.all_to_all(
            copy_grad_up.reshape(n_exp, part_rows, hidden),
            "expert",
            split_axis=0,
            concat_axis=0,
            tiled=True,
        ),
        lax.all_to_all(
            copy_grad_down.reshape(n_exp, part_hidden, width),
            "expert",
            split_axis=0,
            concat_axis=0,
            tiled=True,
        ),
    )
    has_copy = hosted.astype(jnp.bfloat16)[:, None, None]
    owner_grads = (
        lax.all_to_all(
            spread_grads[0][host_dev] * has_copy, "expert", split_axis=0, concat_axis=0, tiled=True
        ),
        lax.all_to_all(
            spread_grads[1][host_dev] * has_copy, "expert", split_axis=0, concat_axis=0, tiled=True
        ),
        lax.all_to_all(
            spread_grads[2][host_dev] * has_copy, "expert", split_axis=0, concat_axis=0, tiled=True
        ),
    )
    grad_gate = (
        matmul_at(home_x, home_dgate) + owner_grads[0].reshape(width, hidden).astype(jnp.float32)
    ).astype(jnp.bfloat16)
    grad_up = (
        matmul_at(home_x, home_dup) + owner_grads[1].reshape(width, hidden).astype(jnp.float32)
    ).astype(jnp.bfloat16)
    grad_down = (
        matmul_at(home_hid, home_d) + owner_grads[2].reshape(hidden, width).astype(jnp.float32)
    ).astype(jnp.bfloat16)
    both = (
        lax.all_to_all(
            home_out.reshape(n_exp, cap, width), "expert", split_axis=0, concat_axis=0, tiled=True
        ),
        lax.all_to_all(
            spill_out.reshape(n_exp, spill, width),
            "expert",
            split_axis=0,
            concat_axis=0,
            tiled=True,
        ),
        lax.all_to_all(
            home_dx.reshape(n_exp, cap, width), "expert", split_axis=0, concat_axis=0, tiled=True
        ),
        lax.all_to_all(
            spill_dx.reshape(n_exp, spill, width), "expert", split_axis=0, concat_axis=0, tiled=True
        ),
    )
    out_back = (both[0], both[1])
    dx_back = (both[2], both[3])
    zero_row = jnp.zeros((1, width), jnp.bfloat16)

    def to_pairs(pair_rows):
        home_rows = jnp.concatenate([pair_rows[0].reshape(home_total, width), zero_row], axis=0)
        spill_rows = jnp.concatenate([pair_rows[1].reshape(spill_total, width), zero_row], axis=0)
        joined = home_rows[home_index].astype(jnp.float32) + spill_rows[spill_index].astype(
            jnp.float32
        )
        return joined.reshape(rows, top, width)

    out_tok = to_pairs(out_back)
    back_tok = to_pairs(dx_back)
    mixed = jnp.sum(gates[:, :, None] * out_tok, axis=1).astype(jnp.bfloat16)
    grad_tokens = jnp.sum(back_tok, axis=1).astype(jnp.bfloat16)
    gate_terms = jnp.sum(cotangent.astype(jnp.float32)[:, None, :] * out_tok, axis=2)
    grad_gates = lax.psum(gate_terms, "dp")
    return (mixed, grad_tokens, grad_gates, grad_gate[None], grad_up[None], grad_down[None])


def solution(mesh):
    placed = (
        P("expert", "dp"),
        P("expert", None),
        P("expert", None),
        P("expert", "dp"),
        P(),
        P("expert", "dp", None),
        P("expert", "dp", None),
        P("expert", None, "dp"),
    )
    return jax.shard_map(
        local,
        mesh=mesh,
        in_specs=placed,
        out_specs=(
            P("expert", "dp"),
            P("expert", "dp"),
            P("expert", None),
            P("expert", "dp", None),
            P("expert", "dp", None),
            P("expert", None, "dp"),
        ),
        check_vma=False,
    )
```

profile of v0, /device:TPU:0, one launch (start us, length us, event | category | flops | bytes accessed | tf_op | source)
XLA Modules:
  0.0 1829.3 jit_solution(10188352927164183435)
XLA Ops:
  39.9 38.5 %all-to-all-done.12 = bf16[16,32,2048]{2,1,0:T(8,128)(2,1)} async-done(((bf16[16,32,2048]{2,1,0:T(8,128)(2,1)}), bf16[16,32,2048]{2,1,0:T(8,128)(2,1)}, u32[]{:S(2)}, u32[]{:S(2)}) %all-to-all-start.12) | async-done | bytes 2097184 | tf_op jit(solution)/shard_map/all_to_all | solution.py:83
  78.4 58.5 %all_to_all.100 = bf16[16,32,2048]{2,1,0:T(8,128)(2,1)} all-to-all(bf16[16,32,2048]{2,1,0:T(8,128)(2,1)S(1)} %bitcast.134), channel_id=1, replica_groups=mesh['dp'=2,'expert'=16] {'expert'}, dimensions={0} | all-to-all | bytes 4194304 | tf_op jit(solution)/shard_map/all_to_all | solution.py:80
  136.9 97.4 %all_to_all.101 = bf16[16,64,2048]{2,1,0:T(8,128)(2,1)} all-to-all(bf16[16,64,2048]{2,1,0:T(8,128)(2,1)S(1)} %bitcast.137), channel_id=1, replica_groups=mesh['dp'=2,'expert'=16] {'expert'}, dimensions={0} | all-to-all | bytes 8388608 | tf_op jit(solution)/shard_map/all_to_all | solution.py:112
  234.3 97.3 %all_to_all.102 = bf16[16,128,1024]{2,1,0:T(8,128)(2,1)} all-to-all(bf16[16,128,1024]{2,1,0:T(8,128)(2,1)S(1)} %bitcast.138), channel_id=1, replica_groups=mesh['dp'=2,'expert'=16] {'expert'}, dimensions={0} | all-to-all | bytes 8388608 | tf_op jit(solution)/shard_map/all_to_all | solution.py:105
  347.4 67.2 %all-to-all-done.3 = bf16[16,128,1024]{2,1,0:T(8,128)(2,1)} async-done(((bf16[16,128,1024]{2,1,0:T(8,128)(2,1)}), bf16[16,128,1024]{2,1,0:T(8,128)(2,1)}, u32[]{:S(2)}, u32[]{:S(2)}) %all-to-all-start.3) | async-done | bytes 4194336 | tf_op jit(solution)/shard_map/all_to_all | solution.py:98
  414.6 19.7 %all-to-all-start = ((bf16[16,64,2048]{2,1,0:T(8,128)(2,1)}), bf16[16,64,2048]{2,1,0:T(8,128)(2,1)}, u32[]{:S(2)}, u32[]{:S(2)}) async-start(bf16[16,64,2048]{2,1,0:T(8,128)(2,1)} %bitcast.133), calls=%async_computation | async-start | bytes 8388608 | tf_op jit(solution)/shard_map/all_to_all | solution.py:74
  449.6 62.2 %all-to-all-done = bf16[16,64,2048]{2,1,0:T(8,128)(2,1)} async-done(((bf16[16,64,2048]{2,1,0:T(8,128)(2,1)}), bf16[16,64,2048]{2,1,0:T(8,128)(2,1)}, u32[]{:S(2)}, u32[]{:S(2)}) %all-to-all-start) | async-done | bytes 4194336 | tf_op jit(solution)/shard_map/all_to_all | solution.py:74
  511.8 19.7 %all-to-all-start.10 = ((bf16[16,64,2048]{2,1,0:T(8,128)(2,1)}), bf16[16,64,2048]{2,1,0:T(8,128)(2,1)}, u32[]{:S(2)}, u32[]{:S(2)}) async-start(bf16[16,64,2048]{2,1,0:T(8,128)(2,1)} %fusion.3), calls=%async_computation.14 | async-start | bytes 8388608 | tf_op jit(solution)/shard_map/all_to_all | solution.py:77
  541.1 67.9 %all-to-all-done.10 = bf16[16,64,2048]{2,1,0:T(8,128)(2,1)} async-done(((bf16[16,64,2048]{2,1,0:T(8,128)(2,1)}), bf16[16,64,2048]{2,1,0:T(8,128)(2,1)}, u32[]{:S(2)}, u32[]{:S(2)}) %all-to-all-start.10) | async-done | bytes 4194336 | tf_op jit(solution)/shard_map/all_to_all | solution.py:77
  609.1 19.7 %all-to-all-start.8 = ((bf16[16,64,2048]{2,1,0:T(8,128)(2,1)}), bf16[16,64,2048]{2,1,0:T(8,128)(2,1)}, u32[]{:S(2)}, u32[]{:S(2)}) async-start(bf16[16,64,2048]{2,1,0:T(8,128)(2,1)} %broadcast_multiply_fusion.3), calls=%async_computation.12 | async-start | bytes 8388608 | tf_op jit(solution)/shard_map/all_to_all | solution.py:125
  646.3 60.0 %all-to-all-done.8 = bf16[16,64,2048]{2,1,0:T(8,128)(2,1)} async-done(((bf16[16,64,2048]{2,1,0:T(8,128)(2,1)}), bf16[16,64,2048]{2,1,0:T(8,128)(2,1)}, u32[]{:S(2)}, u32[]{:S(2)}) %all-to-all-start.8) | async-done | bytes 4194336 | tf_op jit(solution)/shard_map/all_to_all | solution.py:125
  706.3 19.7 %all-to-all-start.4 = ((bf16[16,128,1024]{2,1,0:T(8,128)(2,1)}), bf16[16,128,1024]{2,1,0:T(8,128)(2,1)}, u32[]{:S(2)}, u32[]{:S(2)}) async-start(bf16[16,128,1024]{2,1,0:T(8,128)(2,1)} %get-tuple-element.35), calls=%async_computation.6 | async-start | bytes 8388608 | tf_op jit(solution)/shard_map/all_to_all | solution.py:123
  726.1 9.3 fusion.39
  735.4 9.3 fusion.36
  744.7 58.8 %all-to-all-done.4 = bf16[16,128,1024]{2,1,0:T(8,128)(2,1)} async-done(((bf16[16,128,1024]{2,1,0:T(8,128)(2,1)}), bf16[16,128,1024]{2,1,0:T(8,128)(2,1)}, u32[]{:S(2)}, u32[]{:S(2)}) %all-to-all-start.4) | async-done | bytes 4194336 | tf_op jit(solution)/shard_map/all_to_all | solution.py:123
  803.6 19.7 %all-to-all-start.6 = ((bf16[16,128,1024]{2,1,0:T(8,128)(2,1)}), bf16[16,128,1024]{2,1,0:T(8,128)(2,1)}, u32[]{:S(2)}, u32[]{:S(2)}) async-start(bf16[16,128,1024]{2,1,0:T(8,128)(2,1)} %get-tuple-element.36), calls=%async_computation.9 | async-start | bytes 8388608 | tf_op jit(solution)/shard_map/all_to_all | solution.py:124
  823.3 9.3 fusion.42
  832.9 33.0 %reduce-scatter.15.cloned.1.call-done = bf16[1024,512]{1,0:T(8,128)(2,1)} async-done(((bf16[1024,1024]{1,0:T(8,128)(2,1)}), bf16[1024,512]{1,0:T(8,128)(2,1)}) %reduce-scatter.15.cloned.1.call-update) | async-done | bytes 1048592 | tf_op jit(solution)/shard_map/reduce_scatter | solution.py:137
  870.8 33.2 %all-gather.7.cloned.1.call-done = bf16[1024,1024]{1,0:T(8,128)(2,1)} async-done(((bf16[1024,512]{1,0:T(8,128)(2,1)}), bf16[1024,1024]{1,0:T(8,128)(2,1)}) %all-gather.7.cloned.1.call-update) | async-done | bytes 2097168 | tf_op jit(solution)/shard_map/all_gather | solution.py:156
  904.0 9.3 fusion.22
  921.7 35.2 %all-gather.13.cloned.1.call-done = bf16[1024,1024]{1,0:T(8,128)(2,1)} async-done(((bf16[1024,512]{1,0:T(8,128)(2,1)}), bf16[1024,1024]{1,0:T(8,128)(2,1)}) %all-gather.13.cloned.1.call-update) | async-done | bytes 2097168 | tf_op jit(solution)/shard_map/all_gather | solution.py:158
  957.0 10.9 fusion.14
  974.2 17.8 all-gather.11.cloned.1.call-done
  992.1 11.8 add_convert_fusion
  1003.9 14.0 all-to-all-start.11
  1029.3 15.9 reduce-scatter.13.cloned.1.call-done
  1045.3 23.2 %reduce-scatter.11.cloned.1.call-done = bf16[512,512]{1,0:T(8,128)(2,1)} async-done(((bf16[512,1024]{1,0:T(8,128)(2,1)}), bf16[512,512]{1,0:T(8,128)(2,1)}) %reduce-scatter.11.cloned.1.call-update) | async-done | bytes 524304 | tf_op jit(solution)/shard_map/reduce_scatter | solution.py:140
  1071.8 21.5 %all-gather.9.cloned.1.call-done = bf16[512,1024]{1,0:T(8,128)(2,1)} async-done(((bf16[512,512]{1,0:T(8,128)(2,1)}), bf16[512,1024]{1,0:T(8,128)(2,1)}) %all-gather.9.cloned.1.call-update) | async-done | bytes 1048592 | tf_op jit(solution)/shard_map/all_gather | solution.py:159
  1099.4 15.7 all-to-all-start.9
  1116.4 24.2 %all-gather.15.cloned.1.call-done = bf16[512,1024]{1,0:T(8,128)(2,1)} async-done(((bf16[512,512]{1,0:T(8,128)(2,1)}), bf16[512,1024]{1,0:T(8,128)(2,1)}) %all-gather.15.cloned.1.call-update) | async-done | bytes 1048592 | tf_op jit(solution)/shard_map/all_gather | solution.py:160
  1147.5 16.4 all-gather.17.cloned.1.call-done
  1183.4 35.0 %all-to-all-done.13 = bf16[16,32,2048]{2,1,0:T(8,128)(2,1)} async-done(((bf16[16,32,2048]{2,1,0:T(8,128)(2,1)}), bf16[16,32,2048]{2,1,0:T(8,128)(2,1)}, u32[]{:S(2)}, u32[]{:S(2)}) %all-to-all-start.13) | async-done | bytes 2097184 | tf_op jit(solution)/shard_map/all_to_all | solution.py:231
  1218.4 11.9 all-to-all-start.16
  1234.8 73.1 %all-to-all-done.16 = bf16[16,128,1024]{2,1,0:T(8,128)(2,1)} async-done(((bf16[16,128,1024]{2,1,0:T(8,128)(2,1)}), bf16[16,128,1024]{2,1,0:T(8,128)(2,1)}, u32[]{:S(2)}, u32[]{:S(2)}) %all-to-all-start.16) | async-done | bytes 4194336 | tf_op jit(solution)/shard_map/all_to_all | solution.py:181
  1307.9 19.8 %all-to-all-start.14 = ((bf16[16,128,1024]{2,1,0:T(8,128)(2,1)}), bf16[16,128,1024]{2,1,0:T(8,128)(2,1)}, u32[]{:S(2)}, u32[]{:S(2)}) async-start(bf16[16,128,1024]{2,1,0:T(8,128)(2,1)} %bitcast.143), calls=%async_computation.20 | async-start | bytes 8388608 | tf_op jit(solution)/shard_map/all_to_all | solution.py:174
  1333.7 71.5 %all-to-all-done.14 = bf16[16,128,1024]{2,1,0:T(8,128)(2,1)} async-done(((bf16[16,128,1024]{2,1,0:T(8,128)(2,1)}), bf16[16,128,1024]{2,1,0:T(8,128)(2,1)}, u32[]{:S(2)}, u32[]{:S(2)}) %all-to-all-start.14) | async-done | bytes 4194336 | tf_op jit(solution)/shard_map/all_to_all | solution.py:174
  1405.3 19.8 %all-to-all-start.18 = ((bf16[16,64,2048]{2,1,0:T(8,128)(2,1)}), bf16[16,64,2048]{2,1,0:T(8,128)(2,1)}, u32[]{:S(2)}, u32[]{:S(2)}) async-start(bf16[16,64,2048]{2,1,0:T(8,128)(2,1)} %bitcast.142), calls=%async_computation.24 | async-start | bytes 8388608 | tf_op jit(solution)/shard_map/all_to_all | solution.py:188
  1442.6 60.0 %all-to-all-done.18 = bf16[16,64,2048]{2,1,0:T(8,128)(2,1)} async-done(((bf16[16,64,2048]{2,1,0:T(8,128)(2,1)}), bf16[16,64,2048]{2,1,0:T(8,128)(2,1)}, u32[]{:S(2)}, u32[]{:S(2)}) %all-to-all-start.18) | async-done | bytes 4194336 | tf_op jit(solution)/shard_map/all_to_all | solution.py:188
  1502.6 111.8 %all_to_all.103 = bf16[16,128,1024]{2,1,0:T(8,128)(2,1)} all-to-all(bf16[16,128,1024]{2,1,0:T(8,128)(2,1)} %get-tuple-element.33), channel_id=1, replica_groups=mesh['dp'=2,'expert'=16] {'expert'}, dimensions={0} | all-to-all | bytes 8388608 | tf_op jit(solution)/shard_map/all_to_all | solution.py:201
  1629.5 67.9 %all-to-all-done.15 = bf16[16,128,1024]{2,1,0:T(8,128)(2,1)} async-done(((bf16[16,128,1024]{2,1,0:T(8,128)(2,1)}), bf16[16,128,1024]{2,1,0:T(8,128)(2,1)}, u32[]{:S(2)}, u32[]{:S(2)}) %all-to-all-start.15) | async-done | bytes 4194336 | tf_op jit(solution)/shard_map/all_to_all | solution.py:198
  1697.4 19.9 %all-to-all-start.19 = ((bf16[16,64,2048]{2,1,0:T(8,128)(2,1)}), bf16[16,64,2048]{2,1,0:T(8,128)(2,1)}, u32[]{:S(2)}, u32[]{:S(2)}) async-start(bf16[16,64,2048]{2,1,0:T(8,128)(2,1)} %broadcast_multiply_fusion), calls=%async_computation.25 | async-start | bytes 8388608 | tf_op jit(solution)/shard_map/all_to_all | solution.py:204
  1727.0 11.6 gather_fusion.1
  1738.6 11.6 gather_fusion.8
  1753.8 10.7 gather_fusion.6
  1770.5 8.2 fusion.5
  1795.5 9.1 fusion.6
  1804.6 8.6 fusion.7
  1813.2 9.0 fusion.8
  (168 shorter events, 237.9 us)
Async XLA Ops:
  9.6 14.9 copy-start.15
  9.6 14.9 copy-start.17
  10.6 13.9 copy-start.8
  15.8 418.5 %copy-start.11 = (s32[1024,1]{0,1:T(1,128)}, s32[1024,1]{0,1:T(1,128)S(1)}, u32[]{:S(2)}) copy-start(s32[1024,1]{0,1:T(1,128)S(1)} %get-tuple-element.31) | copy-start | bytes 12292
  28.2 9.2 copy-start.10
  29.9 48.5 %all-to-all-start.12 = ((bf16[16,32,2048]{2,1,0:T(8,128)(2,1)}), bf16[16,32,2048]{2,1,0:T(8,128)(2,1)}, u32[]{:S(2)}, u32[]{:S(2)}) async-start(bf16[16,32,2048]{2,1,0:T(8,128)(2,1)} %fusion.9), calls=%async_computation.17 | async-start | bytes 4194304 | tf_op jit(solution)/shard_map/all_to_all | solution.py:83
  78.4 58.5 %copy-start.2 = (bf16[1,1024,2048]{2,1,0:T(8,128)(2,1)S(1)}, bf16[1,1024,2048]{2,1,0:T(8,128)(2,1)}, u32[]{:S(2)}) copy-start(bf16[1,1024,2048]{2,1,0:T(8,128)(2,1)} %param.15) | copy-start | bytes 12582916
  136.9 97.4 %copy-start.3 = (bf16[1,2048,1024]{2,1,0:T(8,128)(2,1)S(1)}, bf16[1,2048,1024]{2,1,0:T(8,128)(2,1)}, u32[]{:S(2)}) copy-start(bf16[1,2048,1024]{2,1,0:T(8,128)(2,1)} %param.14) | copy-start | bytes 12582916
  331.7 82.9 %all-to-all-start.3 = ((bf16[16,128,1024]{2,1,0:T(8,128)(2,1)}), bf16[16,128,1024]{2,1,0:T(8,128)(2,1)}, u32[]{:S(2)}, u32[]{:S(2)}) async-start(bf16[16,128,1024]{2,1,0:T(8,128)(2,1)} %bitcast.139), calls=%async_computation.5 | async-start | bytes 8388608 | tf_op jit(solution)/shard_map/all_to_all | solution.py:98
  414.6 97.2 %all-to-all-start = ((bf16[16,64,2048]{2,1,0:T(8,128)(2,1)}), bf16[16,64,2048]{2,1,0:T(8,128)(2,1)}, u32[]{:S(2)}, u32[]{:S(2)}) async-start(bf16[16,64,2048]{2,1,0:T(8,128)(2,1)} %bitcast.133), calls=%async_computation | async-start | bytes 8388608 | tf_op jit(solution)/shard_map/all_to_all | solution.py:74
  449.6 81.9 %copy-start.25 = (s32[16]{0:T(128)S(1)}, s32[16]{0:T(128)}, u32[]{:S(2)}) copy-start(s32[16]{0:T(128)} %param.12) | copy-start | bytes 196
  511.8 97.2 %all-to-all-start.10 = ((bf16[16,64,2048]{2,1,0:T(8,128)(2,1)}), bf16[16,64,2048]{2,1,0:T(8,128)(2,1)}, u32[]{:S(2)}, u32[]{:S(2)}) async-start(bf16[16,64,2048]{2,1,0:T(8,128)(2,1)} %fusion.3), calls=%async_computation.14 | async-start | bytes 8388608 | tf_op jit(solution)/shard_map/all_to_all | solution.py:77
  609.1 97.2 %all-to-all-start.8 = ((bf16[16,64,2048]{2,1,0:T(8,128)(2,1)}), bf16[16,64,2048]{2,1,0:T(8,128)(2,1)}, u32[]{:S(2)}, u32[]{:S(2)}) async-start(bf16[16,64,2048]{2,1,0:T(8,128)(2,1)} %broadcast_multiply_fusion.3), calls=%async_computation.12 | async-start | bytes 8388608 | tf_op jit(solution)/shard_map/all_to_all | solution.py:125
  706.3 97.2 %all-to-all-start.4 = ((bf16[16,128,1024]{2,1,0:T(8,128)(2,1)}), bf16[16,128,1024]{2,1,0:T(8,128)(2,1)}, u32[]{:S(2)}, u32[]{:S(2)}) async-start(bf16[16,128,1024]{2,1,0:T(8,128)(2,1)} %get-tuple-element.35), calls=%async_computation.6 | async-start | bytes 8388608 | tf_op jit(solution)/shard_map/all_to_all | solution.py:123
  726.0 106.9 %reduce-scatter.9.cloned.1.call-start = ((), (), s32[]{:S(2)}) async-start(), calls=%async_computation.27 | async-start | bytes 3145728 | tf_op jit(solution)/shard_map/reduce_scatter | solution.py:134
  735.4 97.6 %reduce-scatter.7.cloned.1.call-start = ((), (), s32[]{:S(2)}) async-start(), calls=%async_computation.26 | async-start | bytes 3145728 | tf_op jit(solution)/shard_map/reduce_scatter | solution.py:131
  803.6 109.8 %all-to-all-start.6 = ((bf16[16,128,1024]{2,1,0:T(8,128)(2,1)}), bf16[16,128,1024]{2,1,0:T(8,128)(2,1)}, u32[]{:S(2)}, u32[]{:S(2)}) async-start(bf16[16,128,1024]{2,1,0:T(8,128)(2,1)} %get-tuple-element.36), calls=%async_computation.9 | async-start | bytes 8388608 | tf_op jit(solution)/shard_map/all_to_all | solution.py:124
  823.3 42.7 %reduce-scatter.15.cloned.1.call-start = ((), (), s32[]{:S(2)}) async-start(), calls=%async_computation.32 | async-start | bytes 3145728 | tf_op jit(solution)/shard_map/reduce_scatter | solution.py:137
  832.7 71.4 %all-gather.7.cloned.1.call-start = ((), (), s32[]{:S(2)}) async-start(), calls=%async_computation.28 | async-start | bytes 3145728 | tf_op jit(solution)/shard_map/all_gather | solution.py:156
  913.4 90.5 %all-to-all-start.1 = ((bf16[16,64,2048]{2,1,0:T(8,128)(2,1)}), bf16[16,64,2048]{2,1,0:T(8,128)(2,1)}, u32[]{:S(2)}, u32[]{:S(2)}) async-start(bf16[16,64,2048]{2,1,0:T(8,128)(2,1)} %bitcast.141), calls=%async_computation.3 | async-start | bytes 8388608 | tf_op jit(solution)/shard_map/all_to_all | solution.py:218
  920.5 36.4 %all-gather.13.cloned.1.call-start = ((), (), s32[]{:S(2)}) async-start(), calls=%async_computation.34 | async-start | bytes 3145728 | tf_op jit(solution)/shard_map/all_gather | solution.py:158
  921.1 70.9 %all-gather.11.cloned.1.call-start = ((), (), s32[]{:S(2)}) async-start(), calls=%async_computation.33 | async-start | bytes 3145728 | tf_op jit(solution)/shard_map/all_gather | solution.py:157
  921.7 107.7 %reduce-scatter.17.cloned.1.call-start = ((), (), s32[]{:S(2)}) async-start(), calls=%async_computation.35 | async-start | bytes 1572864 | tf_op jit(solution)/shard_map/reduce_scatter | solution.py:146
  1003.9 14.1 copy-start.6
  1003.9 95.6 %all-to-all-start.11 = ((bf16[16,64,2048]{2,1,0:T(8,128)(2,1)}), bf16[16,64,2048]{2,1,0:T(8,128)(2,1)}, u32[]{:S(2)}, u32[]{:S(2)}) async-start(bf16[16,64,2048]{2,1,0:T(8,128)(2,1)} %bitcast.140), calls=%async_computation.16 | async-start | bytes 8388608 | tf_op jit(solution)/shard_map/all_to_all | solution.py:228
  1017.9 27.4 %reduce-scatter.13.cloned.1.call-start = ((), (), s32[]{:S(2)}) async-start(), calls=%async_computation.30 | async-start | bytes 1572864 | tf_op jit(solution)/shard_map/reduce_scatter | solution.py:143
  1023.5 45.0 %reduce-scatter.11.cloned.1.call-start = ((), (), s32[]{:S(2)}) async-start(), calls=%async_computation.29 | async-start | bytes 1572864 | tf_op jit(solution)/shard_map/reduce_scatter | solution.py:140
  1029.3 64.0 %all-gather.9.cloned.1.call-start = ((), (), s32[]{:S(2)}) async-start(), calls=%async_computation.31 | async-start | bytes 1572864 | tf_op jit(solution)/shard_map/all_gather | solution.py:159
  1099.4 72.0 %all-to-all-start.9 = ((bf16[16,32,2048]{2,1,0:T(8,128)(2,1)}), bf16[16,32,2048]{2,1,0:T(8,128)(2,1)S(1)}, u32[]{:S(2)}, u32[]{:S(2)}) async-start(bf16[16,32,2048]{2,1,0:T(8,128)(2,1)} %bitcast.149), calls=%async_computation.13 | async-start | bytes 4194304 | tf_op jit(solution)/shard_map/all_to_all | solution.py:221
  1115.1 25.6 %all-gather.15.cloned.1.call-start = ((), (), s32[]{:S(2)}) async-start(), calls=%async_computation.36 | async-start | bytes 1572864 | tf_op jit(solution)/shard_map/all_gather | solution.py:160
  1115.8 48.1 %all-gather.17.cloned.1.call-start = ((), (), s32[]{:S(2)}) async-start(), calls=%async_computation.37 | async-start | bytes 1572864 | tf_op jit(solution)/shard_map/all_gather | solution.py:161
  1171.4 12.0 copy-start
  1171.4 47.0 %all-to-all-start.13 = ((bf16[16,32,2048]{2,1,0:T(8,128)(2,1)}), bf16[16,32,2048]{2,1,0:T(8,128)(2,1)}, u32[]{:S(2)}, u32[]{:S(2)}) async-start(bf16[16,32,2048]{2,1,0:T(8,128)(2,1)} %bitcast.150), calls=%async_computation.19 | async-start | bytes 4194304 | tf_op jit(solution)/shard_map/all_to_all | solution.py:231
  1218.4 12.0 copy-start.7
  1218.4 12.0 copy-start.23
  1218.4 89.5 %all-to-all-start.16 = ((bf16[16,128,1024]{2,1,0:T(8,128)(2,1)}), bf16[16,128,1024]{2,1,0:T(8,128)(2,1)}, u32[]{:S(2)}, u32[]{:S(2)}) async-start(bf16[16,128,1024]{2,1,0:T(8,128)(2,1)} %bitcast.144), calls=%async_computation.22 | async-start | bytes 8388608 | tf_op jit(solution)/shard_map/all_to_all | solution.py:181
  1307.9 19.8 %copy-start.22 = (bf16[512,1024]{1,0:T(8,128)(2,1)S(1)}, bf16[512,1024]{1,0:T(8,128)(2,1)}, u32[]{:S(2)}) copy-start(bf16[512,1024]{1,0:T(8,128)(2,1)} %all-gather.9.cloned.1.call-done) | copy-start | bytes 3145732
  1307.9 97.4 %all-to-all-start.14 = ((bf16[16,128,1024]{2,1,0:T(8,128)(2,1)}), bf16[16,128,1024]{2,1,0:T(8,128)(2,1)}, u32[]{:S(2)}, u32[]{:S(2)}) async-start(bf16[16,128,1024]{2,1,0:T(8,128)(2,1)} %bitcast.143), calls=%async_computation.20 | async-start | bytes 8388608 | tf_op jit(solution)/shard_map/all_to_all | solution.py:174
  1405.3 19.8 %copy-start.18 = (s32[16]{0:T(128)S(1)}, s32[16]{0:T(128)}, u32[]{:S(2)}) copy-start(s32[16]{0:T(128)} %copy-done.17) | copy-start | bytes 196
  1405.3 19.9 %copy-start.16 = (s32[16]{0:T(128)S(1)}, s32[16]{0:T(128)}, u32[]{:S(2)}) copy-start(s32[16]{0:T(128)} %copy-done.15) | copy-start | bytes 196
  1405.3 97.4 %all-to-all-start.18 = ((bf16[16,64,2048]{2,1,0:T(8,128)(2,1)}), bf16[16,64,2048]{2,1,0:T(8,128)(2,1)}, u32[]{:S(2)}, u32[]{:S(2)}) async-start(bf16[16,64,2048]{2,1,0:T(8,128)(2,1)} %bitcast.142), calls=%async_computation.24 | async-start | bytes 8388608 | tf_op jit(solution)/shard_map/all_to_all | solution.py:188
  1614.5 82.9 %all-to-all-start.15 = ((bf16[16,128,1024]{2,1,0:T(8,128)(2,1)}), bf16[16,128,1024]{2,1,0:T(8,128)(2,1)}, u32[]{:S(2)}, u32[]{:S(2)}) async-start(bf16[16,128,1024]{2,1,0:T(8,128)(2,1)} %get-tuple-element.34), calls=%async_computation.21 | async-start | bytes 8388608 | tf_op jit(solution)/shard_map/all_to_all | solution.py:198
  1629.5 87.8 %copy-start.5 = (bf16[128,2048]{1,0:T(8,128)(2,1)S(1)}, bf16[128,2048]{1,0:T(8,128)(2,1)}, u32[]{:S(2)}) copy-start(bf16[128,2048]{1,0:T(8,128)(2,1)} %param.11) | copy-start | bytes 1572868
  1629.5 87.9 %copy-start.14 = (s32[1024,1]{0,1:T(1,128)S(1)}, s32[1024,1]{0,1:T(1,128)}, u32[]{:S(2)}) copy-start(s32[1024,1]{0,1:T(1,128)} %copy-done.13) | copy-start | bytes 12292
  1629.5 88.0 %copy-start.12 = (s32[1024,1]{0,1:T(1,128)S(1)}, s32[1024,1]{0,1:T(1,128)}, u32[]{:S(2)}) copy-start(s32[1024,1]{0,1:T(1,128)} %copy-done.11) | copy-start | bytes 12292
  1697.4 115.8 %all-to-all-start.19 = ((bf16[16,64,2048]{2,1,0:T(8,128)(2,1)}), bf16[16,64,2048]{2,1,0:T(8,128)(2,1)}, u32[]{:S(2)}, u32[]{:S(2)}) async-start(bf16[16,64,2048]{2,1,0:T(8,128)(2,1)} %broadcast_multiply_fusion), calls=%async_computation.25 | async-start | bytes 8388608 | tf_op jit(solution)/shard_map/all_to_all | solution.py:204
  1795.5 9.2 copy-start.4
  1795.5 9.2 copy-start.20
  (6 other events, 39.5 us)
Sparse Core Ops, SparseCore 0:
  735.5 33.1 reduce-scatter.8
  770.9 31.8 reduce-scatter.6
  832.8 33.1 reduce-scatter.14
  870.9 33.0 all-gather.6
  922.6 34.3 all-gather.12
  958.9 33.0 all-gather.10
  994.9 20.3 reduce-scatter.16
  1023.6 21.6 reduce-scatter.12
  1048.1 20.3 reduce-scatter.10
  1071.9 21.2 all-gather.8
  1118.0 22.5 all-gather.14
  1142.6 21.2 all-gather.16
where the time goes:
time: 1840 us; the launch traced here: 1830 us
  waiting for transfers between devices  885 us (48%)
  blocking collectives  373 us (20%)
  starting transfers between devices  232 us (13%)
  matrix products  141 us (8%)
  local copies, waits for them, and re-layouts  122 us (7%)
  other arithmetic  61.4 us (3%)
    all_to_all x1, blocking collectives, local(): lax.all_to_all(spread_grads[1][host_dev] * has_copy, 'expert', split_axis...  112 us
    all_to_all x1, blocking collectives, local(): lax.all_to_all(own_down.reshape(n_exp, part_hidden, width), 'expert', spl...  97.4 us
    all_to_all x1, blocking collectives, local(): lax.all_to_all(own_up.reshape(n_exp, part_rows, hidden), 'expert', split_...  97.3 us
    all_to_all x1, waiting for transfers between devices, local(): lax.all_to_all(copy_grad_up.reshape(n_exp, part_rows, hidden), 'expert',...  73.1 us
    all_to_all x1, waiting for transfers between devices, local(): lax.all_to_all(copy_grad_gate.reshape(n_exp, part_rows, hidden), 'expert'...  71.5 us
    all_to_all x1, waiting for transfers between devices, local(): lax.all_to_all(home_d.reshape(n_exp, cap, width), 'expert', split_axis=0,...  67.9 us
    all_to_all x1, waiting for transfers between devices, local(): lax.all_to_all(spread_grads[0][host_dev] * has_copy, 'expert', split_axis...  67.9 us
    all_to_all x1, waiting for transfers between devices, local(): lax.all_to_all(own_gate.reshape(n_exp, part_rows, hidden), 'expert', spli...  67.2 us
  transfers between devices with their start and end apart: 28, of which 20 were waited for; matrix products, arithmetic and copies ran while one was open for 16% of the time, Pallas kernels for 0%

commit v1 on v0

v1 whole, which is shorter than its diff:
```python
import jax
import jax.numpy as jnp
from jax import lax
from jax.sharding import PartitionSpec as P


def dot(left, right, dims):
    return lax.dot_general(left, right, (dims, ((), ())), preferred_element_type=jnp.float32)


def pick(onehot, values):
    rows = lax.dot_general(
        onehot, values, (((2,), (1,)), ((0,), (0,))), preferred_element_type=jnp.float32
    )
    return rows.astype(jnp.bfloat16).reshape(-1, values.shape[2])


def local(tokens, expert_ids, gates, cotangent, partner, w_gate, w_up, w_down):
    n_exp = lax.axis_size("expert")
    n_dp = lax.axis_size("dp")
    me = lax.axis_index("expert")
    rows, width = tokens.shape
    top = expert_ids.shape[1]
    cap = rows * top // n_exp
    slots = cap + cap // 2
    own_gate, own_up, own_down = w_gate[0], w_up[0], w_down[0]

    small = jnp.concatenate([expert_ids.T.astype(jnp.float32), gates.T], axis=0)
    small = lax.all_gather(small, "expert", axis=0, tiled=False)
    all_x = lax.all_gather(tokens, "expert", axis=0, tiled=False)
    all_c = lax.all_gather(cotangent, "expert", axis=0, tiled=False)

    hit = small[:, :top] == me.astype(jnp.float32)
    present = jnp.any(hit, axis=1)
    token_gate = jnp.sum(jnp.where(hit, small[:, top:], 0.0), axis=1)
    order = jnp.arange(rows)
    earlier = (order[:, None] < order[None, :]).astype(jnp.bfloat16)
    rank = dot(present.astype(jnp.bfloat16), earlier, ((1,), (0,))).astype(jnp.int32)
    limit = jnp.where(jnp.any(partner == me), slots, cap)
    taken = jnp.logical_and(present, rank < limit)
    place = jnp.where(taken, rank, -1)
    match = place[:, None, :] == jnp.arange(slots)[None, :, None]
    onehot = match.astype(jnp.bfloat16)
    slot_gate = jnp.sum(jnp.where(match, token_gate[:, None, :], 0.0), axis=2).reshape(-1, 1)
    back = (jnp.arange(slots)[None, None, :] == place[:, :, None]).astype(jnp.bfloat16)

    xs = pick(onehot, all_x)
    pre_g = dot(xs, own_gate, ((1,), (0,))).astype(jnp.bfloat16)
    pre_u = dot(xs, own_up, ((1,), (0,))).astype(jnp.bfloat16)
    cs = pick(onehot, all_c)
    pre_d = dot(cs, own_down, ((1,), (1,))).astype(jnp.bfloat16)

    if n_dp == 2:
        swap = [(0, 1), (1, 0)]

        def summed(part):
            other = lax.ppermute(part, "dp", swap)
            return part.astype(jnp.float32) + other.astype(jnp.float32)

        def full(part):
            return part
    else:

        def summed(part):
            part = lax.psum_scatter(part, "dp", scatter_dimension=1, tiled=True)
            return part.astype(jnp.float32)

        def full(part):
            return lax.all_gather(part, "dp", axis=1, tiled=True)

    gate_pre = summed(pre_g)
    up_pre = summed(pre_u)
    sig = jax.nn.sigmoid(gate_pre)
    act = gate_pre * sig
    hid = act * up_pre
    scaled_hid = full((slot_gate * hid).astype(jnp.bfloat16))

    def send_home(slot_rows):
        parts = pick(back, slot_rows.reshape(n_exp, slots, width))
        return lax.psum_scatter(parts, "expert", scatter_dimension=0, tiled=True)

    out = dot(scaled_hid, own_down, ((1,), (0,))).astype(jnp.bfloat16)
    mixed = send_home(out)

    raw = summed(pre_d)
    dhid = slot_gate * raw
    dup = full((dhid * act).astype(jnp.bfloat16))
    dgate = full((dhid * up_pre * sig * (1.0 + gate_pre * (1.0 - sig))).astype(jnp.bfloat16))
    slot_terms = jnp.sum(hid * raw, axis=1).reshape(n_exp, 1, slots)
    dx = (dot(dgate, own_gate, ((1,), (1,))) + dot(dup, own_up, ((1,), (1,)))).astype(jnp.bfloat16)
    grad_tokens = send_home(dx)

    mine = place[:, :, None] == jnp.arange(slots)[None, None, :]
    terms = jnp.sum(jnp.where(mine, slot_terms, 0.0), axis=2)
    terms = lax.all_to_all(terms, "expert", split_axis=0, concat_axis=0, tiled=True)
    labels = jnp.arange(n_exp, dtype=jnp.int32)
    chosen = expert_ids.T[None, :, :] == labels[:, None, None]
    grad_gates = jnp.sum(jnp.where(chosen, terms[:, None, :], 0.0), axis=0).T
    if n_dp != 2:
        grad_gates = lax.psum(grad_gates, "dp")

    grad_down = dot(scaled_hid, cs, ((0,), (0,))).astype(jnp.bfloat16)
    grad_up = dot(xs, dup, ((0,), (0,))).astype(jnp.bfloat16)
    grad_gate = dot(xs, dgate, ((0,), (0,))).astype(jnp.bfloat16)
    return (mixed, grad_tokens, grad_gates, grad_gate[None], grad_up[None], grad_down[None])


def solution(mesh):
    placed = (
        P("expert", "dp"),
        P("expert", None),
        P("expert", None),
        P("expert", "dp"),
        P(),
        P("expert", "dp", None),
        P("expert", "dp", None),
        P("expert", None, "dp"),
    )
    return jax.shard_map(
        local,
        mesh=mesh,
        in_specs=placed,
        out_specs=(
            P("expert", "dp"),
            P("expert", "dp"),
            P("expert", None),
            P("expert", "dp", None),
            P("expert", "dp", None),
            P("expert", None, "dp"),
        ),
        check_vma=False,
    )
```

time: 1840 us -> 633 us (0.34)
  waiting for transfers between devices: 885 us -> 458 us
  blocking collectives: 373 us -> 24.3 us
  starting transfers between devices: 232 us -> 7.37 us
  local copies, waits for them, and re-layouts: 122 us -> 0.22 us
  other arithmetic: 61.4 us -> 15.2 us
  matrix products: 141 us -> 110 us
    all_to_all x16 -> x1, waiting for transfers between devices: 662 us -> 0.01 us  [local(): lax.all_to_all(terms, 'expert', split_axis=0, concat_axis=0, tiled=True)]
    all_to_all x4 -> x0, blocking collectives: 365 us -> none  [the longest x1 112 us: local(): lax.all_to_all(spread_grads[1][host_dev] * has_copy, 'expert', split_axis...]
    all_to_all x16 -> x1, starting transfers between devices: 231 us -> 3.74 us  [local(): lax.all_to_all(terms, 'expert', split_axis=0, concat_axis=0, tiled=True)]
    ppermute x0 -> x3, waiting for transfers between devices: none -> 193 us  [summed(): other = lax.ppermute(part, 'dp', swap)]
    gather x14 -> x0, local copies, waits for them, and re-layouts: 86.7 us -> none  [the longest x2 23.1 us: to_pairs(): home_rows[home_index].astype(jnp.float32)]
    reduce_scatter x6 -> x2, waiting for transfers between devices: 72.3 us -> 145 us  [send_home(): return lax.psum_scatter(parts, 'expert', scatter_dimension=0, tiled=True)]
    dot_general x18 -> x14, matrix products: 141 us -> 110 us  [the longest x10 85.6 us: dot(): lax.dot_general(left, right, (dims, ((), ())), preferred_element_type=jnp...]
    all_gather x6 -> x2, waiting for transfers between devices: 148 us -> 118 us  [the longest x1 67.3 us: local(): all_x = lax.all_gather(tokens, 'expert', axis=0, tiled=False)]
  transfers between devices with their start and end apart: 28 -> 8, of which waited for: 20 -> 7; matrix products, arithmetic and copies ran while one was open for 16% -> 13% of each run, Pallas kernels for 0% -> 0%
where the time goes in v1:
time: 633 us; the launch traced here: 629 us
  waiting for transfers between devices  458 us (72%)
  matrix products  110 us (17%)
  blocking collectives  24.3 us (4%)
  other arithmetic  15.2 us (2%)
  between operations  14.9 us (2%)
  starting transfers between devices  7.37 us (1%)
    ppermute x3, waiting for transfers between devices, summed(): other = lax.ppermute(part, 'dp', swap)  193 us
    reduce_scatter x2, waiting for transfers between devices, send_home(): return lax.psum_scatter(parts, 'expert', scatter_dimension=0, tiled=True)  145 us
    dot_general x10, matrix products, dot(): lax.dot_general(left, right, (dims, ((), ())), preferred_element_type=jnp...  85.6 us
    all_gather x1, waiting for transfers between devices, local(): all_x = lax.all_gather(tokens, 'expert', axis=0, tiled=False)  67.3 us
    all_gather x1, waiting for transfers between devices, local(): all_c = lax.all_gather(cotangent, 'expert', axis=0, tiled=False)  51 us
    all_gather x1, blocking collectives, local(): small = lax.all_gather(small, 'expert', axis=0, tiled=False)  24.3 us
    dot_general x4, matrix products, pick(): lax.dot_general(onehot, values, (((2,), (1,)), ((0,), (0,))), preferred_e...  24.3 us
  transfers between devices with their start and end apart: 8, of which 7 were waited for; matrix products, arithmetic and copies ran while one was open for 13% of the time, Pallas kernels for 0%

profile of v1, /device:TPU:0, one launch (start us, length us, event | category | flops | bytes accessed | tf_op | source)
XLA Modules:
  0.0 629.4 jit_solution(4907961785617172263)
XLA Ops:
  7.2 0.0 all-gather.8.cloned.1.call-start
  7.2 0.7 all-gather.8.cloned.1.call-update
  7.9 0.0 all-gather.6.cloned.1.call-start
  7.9 0.7 all-gather.6.cloned.1.call-update
  8.6 0.0 reduce-scatter.3.cloned.1.call-start
  8.7 1.3 compare_reduce_fusion
  10.6 0.7 bitcast_convert_fusion
  11.3 0.7 pad_maximum_fusion
  12.0 24.3 %all-gather = f32[256,128]{1,0:T(8,128)S(1)} all-gather(f32[16,128]{1,0:T(8,128)S(1)} %pad_maximum_fusion), channel_id=2, replica_groups=mesh['dp'=2,'expert'=16] {'expert'}, dimensions={0}, use_global_device_ids=true | all-gather | bytes 139264 | tf_op jit(solution)/shard_map/all_gather | solution.py:29
  36.4 0.1 and_select_fusion
  36.5 51.0 %all-gather.8.cloned.1.call-done = bf16[2048,2048]{1,0:T(8,128)(2,1)} async-done(((bf16[128,2048]{1,0:T(8,128)(2,1)}), bf16[2048,2048]{1,0:T(8,128)(2,1)}) %all-gather.8.cloned.1.call-update) | async-done | bytes 8388624 | tf_op jit(solution)/shard_map/all_gather | solution.py:31
  87.5 7.8 %convolution_convert_fusion.3 = bf16[16,96,2048]{2,1,0:T(8,128)(2,1)} fusion(bf16[16,128,2048]{2,1,0:T(8,128)(2,1)} %bitcast.61, s32[16,128]{1,0:T(8,128)S(1)} %and_select_fusion), kind=kOutput, calls=%fused_computation.15 | convolution fusion | flops 808648704 | bytes 14688256 | tf_op jit(solution)/shard_map/dot_general | solution.py:12
  95.4 67.3 %all-gather.6.cloned.1.call-done = bf16[2048,2048]{1,0:T(8,128)(2,1)} async-done(((bf16[128,2048]{1,0:T(8,128)(2,1)}), bf16[2048,2048]{1,0:T(8,128)(2,1)}) %all-gather.6.cloned.1.call-update) | async-done | bytes 8388624 | tf_op jit(solution)/shard_map/all_gather | solution.py:30
  162.6 5.3 convolution_convert_fusion.4
  168.0 0.0 copy-start.9
  168.0 7.6 %fusion.16 = bf16[1536,1024]{0,1:T(8,128)(2,1)S(1)} fusion(bf16[1536,2048]{1,0:T(8,128)(2,1)S(1)} %bitcast.69, bf16[1,2048,1024]{2,1,0:T(8,128)(2,1)S(1)} %copy-done.10), kind=kOutput, calls=%fused_computation.31 | convolution fusion | flops 6444023808 | bytes 13631488 | tf_op jit(solution)/shard_map/dot_general | solution.py:8
  175.6 0.0 copy-start.5
  175.6 0.0 copy-start.7
  175.6 8.2 %fusion.13 = bf16[1536,1024]{0,1:T(8,128)(2,1)} fusion(bf16[1536,2048]{1,0:T(8,128)(2,1)S(1)} %bitcast.70, bf16[1,2048,1024]{2,1,0:T(8,128)(2,1)S(1)} %copy-done.9), kind=kOutput, calls=%fused_computation.30 | convolution fusion | flops 6444023808 | bytes 13631488 | tf_op jit(solution)/shard_map/dot_general | solution.py:8
  183.8 1.5 collective-permute-start
  185.2 0.6 collective-permute-start.1
  185.8 8.1 %fusion.19 = bf16[1536,1024]{0,1:T(8,128)(2,1)} fusion(bf16[1536,2048]{1,0:T(8,128)(2,1)S(1)} %bitcast.65, bf16[1,1024,2048]{2,1,0:T(8,128)(2,1)S(1)} %copy-done.7), kind=kOutput, calls=%fused_computation.32 | convolution fusion | flops 6444023808 | bytes 13631488 | tf_op jit(solution)/shard_map/dot_general | solution.py:8
  193.9 1.5 collective-permute-start.2
  195.3 0.4 select_reduce_fusion.1
  195.7 0.1 mul.40
  195.8 59.3 %collective-permute-done = bf16[1536,1024]{0,1:T(8,128)(2,1)} collective-permute-done((bf16[1536,1024]{0,1:T(8,128)(2,1)}, bf16[1536,1024]{0,1:T(8,128)(2,1)}, u32[]{:S(2)}, u32[]{:S(2)}) %collective-permute-start) | collective-permute-done | bytes 3145760 | tf_op jit(solution)/shard_map/ppermute | solution.py:57
  255.1 67.4 %collective-permute-done.1 = bf16[1536,1024]{0,1:T(8,128)(2,1)} collective-permute-done((bf16[1536,1024]{0,1:T(8,128)(2,1)S(1)}, bf16[1536,1024]{0,1:T(8,128)(2,1)}, u32[]{:S(2)}, u32[]{:S(2)}) %collective-permute-start.1) | collective-permute-done | bytes 3145760 | tf_op jit(solution)/shard_map/ppermute | solution.py:57
  322.5 66.7 %collective-permute-done.2 = bf16[1536,1024]{0,1:T(8,128)(2,1)} collective-permute-done((bf16[1536,1024]{0,1:T(8,128)(2,1)}, bf16[1536,1024]{0,1:T(8,128)(2,1)}, u32[]{:S(2)}, u32[]{:S(2)}) %collective-permute-start.2) | collective-permute-done | bytes 3145760 | tf_op jit(solution)/shard_map/ppermute | solution.py:57
  389.1 10.7 %multiply_reduce_fusion = (f32[1536]{0:T(1024)S(1)}, bf16[1536,1024]{0,1:T(8,128)(2,1)}, bf16[1536,1024]{0,1:T(8,128)(2,1)S(1)}, bf16[1536,1024]{0,1:T(8,128)(2,1)S(1)}) fusion(bf16[1536,1024]{0,1:T(8,128)(2,1)} %collective-permute-done.2, bf16[1536,1024]{0,1:T(8,128)(2,1)} %fusion.19, bf16[1536,1024]{0,1:T(8,128)(2,1)} %collective-permute-done.1, ...), kind=kLoop, calls=%fused_computation.2 | loop fusion | flops 44038656 | bytes 28323840 | tf_op jit(solution)/shard_map/reduce_sum | solution.py:89
  399.8 7.2 %convolution_convert_fusion = bf16[1536,2048]{1,0:T(8,128)(2,1)S(1)} fusion(bf16[1536,1024]{0,1:T(8,128)(2,1)S(1)} %get-tuple-element.10, bf16[1,1024,2048]{2,1,0:T(8,128)(2,1)S(1)} %copy-done.8), kind=kOutput, calls=%fused_computation.1 | convolution fusion | flops 6445596672 | bytes 13631488 | tf_op jit(solution)/shard_map/dot_general | solution.py:8
  407.0 5.6 convolution_convert_fusion.2
  412.6 0.0 reduce-scatter.3.cloned.1.call-update
  412.6 0.0 reduce-scatter.5.cloned.1.call-start
  412.7 0.0 copy-start.11
  412.7 12.8 %fusion.9 = f32[1536,2048]{1,0:T(8,128)} fusion(bf16[1536,1024]{0,1:T(8,128)(2,1)} %get-tuple-element.9, bf16[1,2048,1024]{2,1,0:T(8,128)(2,1)} %param.13), kind=kOutput, calls=%fused_computation.23 | convolution fusion | flops 6442450944 | bytes 19922944 | tf_op jit(solution)/shard_map/dot_general | solution.py:8
  425.4 10.4 %add_convert_fusion = bf16[1536,2048]{1,0:T(8,128)(2,1)S(1)} fusion(f32[1536,2048]{1,0:T(8,128)} %fusion.9, bf16[1536,1024]{0,1:T(8,128)(2,1)S(1)} %get-tuple-element.11, bf16[1,2048,1024]{2,1,0:T(8,128)(2,1)S(1)} %copy-done.11), kind=kOutput, calls=%fused_computation | convolution fusion | flops 6448742400 | bytes 26214400 | tf_op jit(solution)/shard_map/dot_general | solution.py:8
  435.9 5.6 convolution_convert_fusion.1
  441.5 0.0 reduce-scatter.5.cloned.1.call-update
  441.5 0.1 broadcast_in_dim.71
  441.6 0.9 select_reduce_fusion
  442.4 3.7 all-to-all-start
  446.2 0.0 copy-start.4
  446.2 11.8 %convert_bitcast_fusion.2 = bf16[1,2048,1024]{2,1,0:T(8,128)(2,1)} fusion(bf16[1536,2048]{1,0:T(8,128)(2,1)} %bitcast.71, bf16[1536,1024]{0,1:T(8,128)(2,1)} %get-tuple-element.9), kind=kOutput, calls=%fused_computation.29 | convolution fusion | flops 6444548096 | bytes 13631488 | tf_op jit(solution)/shard_map/dot_general | solution.py:8
  458.0 11.3 %convert_bitcast_fusion.1 = bf16[1,2048,1024]{2,1,0:T(8,128)(2,1)} fusion(bf16[1536,2048]{1,0:T(8,128)(2,1)} %bitcast.72, bf16[1536,1024]{0,1:T(8,128)(2,1)S(1)} %copy-done.4), kind=kOutput, calls=%fused_computation.28 | convolution fusion | flops 6444548096 | bytes 13631488 | tf_op jit(solution)/shard_map/dot_general | solution.py:8
  469.3 8.2 %convert_bitcast_fusion = bf16[1,1024,2048]{2,1,0:T(8,128)(2,1)} fusion(bf16[1536,1024]{0,1:T(8,128)(2,1)S(1)} %copy-done.2, bf16[1536,2048]{1,0:T(8,128)(2,1)S(1)} %bitcast.68), kind=kOutput, calls=%fused_computation.27 | convolution fusion | flops 6444548096 | bytes 13631488 | tf_op jit(solution)/shard_map/dot_general | solution.py:8
  477.5 0.6 select_reduce_fusion.2
  478.1 36.9 %reduce-scatter.3.cloned.1.call-done = bf16[128,2048]{1,0:T(8,128)(2,1)} async-done(((bf16[2048,2048]{1,0:T(8,128)(2,1)}), bf16[128,2048]{1,0:T(8,128)(2,1)}) %reduce-scatter.3.cloned.1.call-update) | async-done | bytes 524304 | tf_op jit(solution)/shard_map/reduce_scatter | solution.py:80
  515.0 107.6 %reduce-scatter.5.cloned.1.call-done = bf16[128,2048]{1,0:T(8,128)(2,1)} async-done(((bf16[2048,2048]{1,0:T(8,128)(2,1)}), bf16[128,2048]{1,0:T(8,128)(2,1)}) %reduce-scatter.5.cloned.1.call-update) | async-done | bytes 524304 | tf_op jit(solution)/shard_map/reduce_scatter | solution.py:80
  (32 shorter events, 0.1 us)
Async XLA Ops:
  7.2 80.4 %all-gather.8.cloned.1.call-start = ((), (), s32[]{:S(2)}) async-start(), calls=%async_computation.6 | async-start | bytes 8912896 | tf_op jit(solution)/shard_map/all_gather | solution.py:31
  7.9 154.7 %all-gather.6.cloned.1.call-start = ((), (), s32[]{:S(2)}) async-start(), calls=%async_computation.5 | async-start | bytes 8912896 | tf_op jit(solution)/shard_map/all_gather | solution.py:30
  8.6 506.4 %reduce-scatter.3.cloned.1.call-start = ((), (), s32[]{:S(2)}) async-start(), calls=%async_computation.3 | async-start | bytes 8912896 | tf_op jit(solution)/shard_map/reduce_scatter | solution.py:80
  162.6 5.3 copy-start.10
  167.9 7.6 %copy-start = (bf16[16,96,2048]{2,1,0:T(8,128)(2,1)}, bf16[16,96,2048]{2,1,0:T(8,128)(2,1)S(1)}, u32[]{:S(2)}) copy-start(bf16[16,96,2048]{2,1,0:T(8,128)(2,1)S(1)} %convolution_convert_fusion.4) | copy-start | bytes 18874372
  168.0 7.6 %copy-start.9 = (bf16[1,2048,1024]{2,1,0:T(8,128)(2,1)S(1)}, bf16[1,2048,1024]{2,1,0:T(8,128)(2,1)}, u32[]{:S(2)}) copy-start(bf16[1,2048,1024]{2,1,0:T(8,128)(2,1)} %param.13) | copy-start | bytes 12582916
  168.0 17.8 %slice-start = ((s8[6291456]{0:T(1024)(128)(4,1)}), s8[4194304]{0:T(1024)(128)(4,1)S(1)}, s32[]{:S(2)}) async-start(s8[6291456]{0:T(1024)(128)(4,1)} %bitcast.63), calls=%async_computation.7 | async-start | bytes 8388608
  175.6 9.7 %copy-start.5 = (bf16[1536,1024]{0,1:T(8,128)(2,1)}, bf16[1536,1024]{0,1:T(8,128)(2,1)S(1)}, u32[]{:S(2)}) copy-start(bf16[1536,1024]{0,1:T(8,128)(2,1)S(1)} %fusion.16) | copy-start | bytes 9437188
  175.6 10.2 %slice-start.1 = ((s8[6291456]{0:T(1024)(128)(4,1)}), s8[2097152]{0:T(1024)(128)(4,1)S(1)}, s32[]{:S(2)}) async-start(s8[6291456]{0:T(1024)(128)(4,1)} %bitcast.63), calls=%async_computation.8 | async-start | bytes 4194304
  175.6 10.2 %copy-start.7 = (bf16[1,1024,2048]{2,1,0:T(8,128)(2,1)S(1)}, bf16[1,1024,2048]{2,1,0:T(8,128)(2,1)}, u32[]{:S(2)}) copy-start(bf16[1,1024,2048]{2,1,0:T(8,128)(2,1)} %param.15) | copy-start | bytes 12582916
  183.8 71.3 %collective-permute-start = (bf16[1536,1024]{0,1:T(8,128)(2,1)}, bf16[1536,1024]{0,1:T(8,128)(2,1)}, u32[]{:S(2)}, u32[]{:S(2)}) collective-permute-start(bf16[1536,1024]{0,1:T(8,128)(2,1)} %fusion.13), channel_id=1, source_target_pairs={{0,16},{16,0},{1,17},{17,1},{2,18},{18,2},{3,19},{19,3},{4,20},{20... | collective-permute-start | bytes 9437192 | tf_op jit(solution)/shard_map/ppermute | solution.py:57
  185.2 137.2 %collective-permute-start.1 = (bf16[1536,1024]{0,1:T(8,128)(2,1)S(1)}, bf16[1536,1024]{0,1:T(8,128)(2,1)}, u32[]{:S(2)}, u32[]{:S(2)}) collective-permute-start(bf16[1536,1024]{0,1:T(8,128)(2,1)S(1)} %fusion.16), channel_id=1, source_target_pairs={{0,16},{16,0},{1,17},{17,1},{2,18},{18,2},{3,19},{19,3},{4,20},{20... | collective-permute-start | bytes 9437192 | tf_op jit(solution)/shard_map/ppermute | solution.py:57
  193.9 195.3 %collective-permute-start.2 = (bf16[1536,1024]{0,1:T(8,128)(2,1)}, bf16[1536,1024]{0,1:T(8,128)(2,1)}, u32[]{:S(2)}, u32[]{:S(2)}) collective-permute-start(bf16[1536,1024]{0,1:T(8,128)(2,1)} %fusion.19), channel_id=1, source_target_pairs={{0,16},{16,0},{1,17},{17,1},{2,18},{18,2},{3,19},{19,3},{4,20},{20... | collective-permute-start | bytes 9437192 | tf_op jit(solution)/shard_map/ppermute | solution.py:57
  195.8 204.0 %copy-start.8 = (bf16[1,1024,2048]{2,1,0:T(8,128)(2,1)S(1)}, bf16[1,1024,2048]{2,1,0:T(8,128)(2,1)}, u32[]{:S(2)}) copy-start(bf16[1,1024,2048]{2,1,0:T(8,128)(2,1)} %param.15) | copy-start | bytes 12582916
  399.8 7.2 %copy-start.1 = (bf16[1536,1024]{0,1:T(8,128)(2,1)}, bf16[1536,1024]{0,1:T(8,128)(2,1)S(1)}, u32[]{:S(2)}) copy-start(bf16[1536,1024]{0,1:T(8,128)(2,1)S(1)} %get-tuple-element.10) | copy-start | bytes 9437188
  399.8 25.6 %copy-start.3 = (bf16[1536,1024]{0,1:T(8,128)(2,1)}, bf16[1536,1024]{0,1:T(8,128)(2,1)S(1)}, u32[]{:S(2)}) copy-start(bf16[1536,1024]{0,1:T(8,128)(2,1)S(1)} %get-tuple-element.11) | copy-start | bytes 9437188
  412.6 210.0 %reduce-scatter.5.cloned.1.call-start = ((), (), s32[]{:S(2)}) async-start(), calls=%async_computation.4 | async-start | bytes 8912896 | tf_op jit(solution)/shard_map/reduce_scatter | solution.py:80
  412.7 12.8 %copy-start.11 = (bf16[1,2048,1024]{2,1,0:T(8,128)(2,1)S(1)}, bf16[1,2048,1024]{2,1,0:T(8,128)(2,1)}, u32[]{:S(2)}) copy-start(bf16[1,2048,1024]{2,1,0:T(8,128)(2,1)} %param.14) | copy-start | bytes 12582916
  441.5 27.8 %slice-start.2 = ((s8[6291456]{0:T(1024)(128)(4,1)}), s8[2097152]{0:T(1024)(128)(4,1)S(1)}, s32[]{:S(2)}) async-start(s8[6291456]{0:T(1024)(128)(4,1)} %bitcast.66), calls=%async_computation.9 | async-start | bytes 4194304
  442.4 35.1 %all-to-all-start = ((f32[16,1,128]{2,1,0:T(1,128)}), f32[16,1,128]{2,1,0:T(1,128)S(1)}, u32[]{:S(2)}, u32[]{:S(2)}) async-start(f32[16,1,128]{2,1,0:T(1,128)} %bitcast.14), calls=%async_computation.2 | async-start | bytes 16384 | tf_op jit(solution)/shard_map/all_to_all | solution.py:95
  446.2 11.8 %copy-start.4 = (bf16[1536,1024]{0,1:T(8,128)(2,1)S(1)}, bf16[1536,1024]{0,1:T(8,128)(2,1)}, u32[]{:S(2)}) copy-start(bf16[1536,1024]{0,1:T(8,128)(2,1)} %copy-done.3) | copy-start | bytes 9437188
  446.2 23.1 %slice-start.3 = ((s8[6291456]{0:T(1024)(128)(4,1)}), s8[4194304]{0:T(1024)(128)(4,1)S(1)}, s32[]{:S(2)}) async-start(s8[6291456]{0:T(1024)(128)(4,1)} %bitcast.66), calls=%async_computation.10 | async-start | bytes 8388608
  458.0 11.3 %copy-start.2 = (bf16[1536,1024]{0,1:T(8,128)(2,1)S(1)}, bf16[1536,1024]{0,1:T(8,128)(2,1)}, u32[]{:S(2)}) copy-start(bf16[1536,1024]{0,1:T(8,128)(2,1)} %copy-done.1) | copy-start | bytes 9437188
  469.3 8.2 %copy-start.6 = (s32[128,8]{0,1:T(8,128)S(1)}, s32[128,8]{0,1:T(8,128)}, u32[]{:S(2)}) copy-start(s32[128,8]{0,1:T(8,128)} %param.9) | copy-start | bytes 12292
Sparse Core Ops, SparseCore 0:
  10.1 77.3 all-gather.7
  89.7 72.8 all-gather.5
  412.7 102.2 reduce-scatter.2
  519.5 103.1 reduce-scatter.4

commit v2 on v1

--- a/solution.py
+++ b/solution.py
@@ -28,7 +28,8 @@
     small = jnp.concatenate([expert_ids.T.astype(jnp.float32), gates.T], axis=0)
     small = lax.all_gather(small, "expert", axis=0, tiled=False)
     all_x = lax.all_gather(tokens, "expert", axis=0, tiled=False)
-    all_c = lax.all_gather(cotangent, "expert", axis=0, tiled=False)
+    later, all_x = lax.optimization_barrier((cotangent, all_x))
+    all_c = lax.all_gather(later, "expert", axis=0, tiled=False)
 
     hit = small[:, :top] == me.astype(jnp.float32)
     present = jnp.any(hit, axis=1)
@@ -53,42 +54,59 @@
     if n_dp == 2:
         swap = [(0, 1), (1, 0)]
 
-        def summed(part):
-            other = lax.ppermute(part, "dp", swap)
-            return part.astype(jnp.float32) + other.astype(jnp.float32)
+        def exchange(part):
+            return (part, lax.ppermute(part, "dp", swap))
+
+        def summed(both):
+            return both[0].astype(jnp.float32) + both[1].astype(jnp.float32)
 
         def full(part):
             return part
     else:
 
-        def summed(part):
-            part = lax.psum_scatter(part, "dp", scatter_dimension=1, tiled=True)
-            return part.astype(jnp.float32)
+        def exchange(part):
+            return (lax.psum_scatter(part, "dp", scatter_dimension=1, tiled=True),)
+
+        def summed(both):
+            return both[0].astype(jnp.float32)
 
         def full(part):
             return lax.all_gather(part, "dp", axis=1, tiled=True)
 
-    gate_pre = summed(pre_g)
-    up_pre = summed(pre_u)
+    sum_g = exchange(pre_g)
+    sum_u = exchange(pre_u)
+    sum_d = exchange(pre_d)
+    sum_g, sum_u, _ = lax.optimization_barrier((sum_g, sum_u, pre_d))
+    gate_pre = summed(sum_g)
+    up_pre = summed(sum_u)
     sig = jax.nn.sigmoid(gate_pre)
     act = gate_pre * sig
     hid = act * up_pre
     scaled_hid = full((slot_gate * hid).astype(jnp.bfloat16))
 
-    def send_home(slot_rows):
-        parts = pick(back, slot_rows.reshape(n_exp, slots, width))
+    def to_tokens(slot_rows):
+        return pick(back, slot_rows.reshape(n_exp, slots, width))
+
+    def send_home(parts):
         return lax.psum_scatter(parts, "expert", scatter_dimension=0, tiled=True)
 
     out = dot(scaled_hid, own_down, ((1,), (0,))).astype(jnp.bfloat16)
-    mixed = send_home(out)
+    out_parts = to_tokens(out)
+    mixed = send_home(out_parts)
 
-    raw = summed(pre_d)
+    sum_d, sum_g, sum_u, _ = lax.optimization_barrier((sum_d, sum_g, sum_u, out_parts))
+    gate_pre = summed(sum_g)
+    up_pre = summed(sum_u)
+    sig = jax.nn.sigmoid(gate_pre)
+    act = gate_pre * sig
+    hid = act * up_pre
+    raw = summed(sum_d)
     dhid = slot_gate * raw
     dup = full((dhid * act).astype(jnp.bfloat16))
     dgate = full((dhid * up_pre * sig * (1.0 + gate_pre * (1.0 - sig))).astype(jnp.bfloat16))
     slot_terms = jnp.sum(hid * raw, axis=1).reshape(n_exp, 1, slots)
     dx = (dot(dgate, own_gate, ((1,), (1,))) + dot(dup, own_up, ((1,), (1,)))).astype(jnp.bfloat16)
-    grad_tokens = send_home(dx)
+    grad_tokens = send_home(to_tokens(dx))
 
     mine = place[:, :, None] == jnp.arange(slots)[None, None, :]
     terms = jnp.sum(jnp.where(mine, slot_terms, 0.0), axis=2)

time: 633 us -> 507 us (0.80)
  waiting for transfers between devices: 458 us -> 338 us
    reduce_scatter x2, waiting for transfers between devices: 145 us -> 67.5 us  [send_home(): return lax.psum_scatter(parts, 'expert', scatter_dimension=0, tiled=True)]
    ppermute x3, waiting for transfers between devices: 193 us -> 162 us  [exchange(): return (part, lax.ppermute(part, 'dp', swap))]
    all_gather x1, waiting for transfers between devices: 51 us -> 28.5 us  [local(): all_c = lax.all_gather(later, 'expert', axis=0, tiled=False)]
    all_gather x1, waiting for transfers between devices: 67.3 us -> 79.2 us  [local(): all_x = lax.all_gather(tokens, 'expert', axis=0, tiled=False)]
    convert_element_type x0 -> x1, other arithmetic: none -> 6.53 us  [local(): scaled_hid = full((slot_gate * hid).astype(jnp.bfloat16))]
  transfers between devices with their start and end apart: 8 -> 8, of which waited for: 7 -> 6; matrix products, arithmetic and copies ran while one was open for 13% -> 21% of each run, Pallas kernels for 0% -> 0%
where the time goes in v2:
time: 507 us; the launch traced here: 504 us
  waiting for transfers between devices  338 us (67%)
  matrix products  104 us (21%)
  other arithmetic  20.5 us (4%)
  blocking collectives  20 us (4%)
  between operations  14.9 us (3%)
  starting transfers between devices  7.17 us (1%)
    ppermute x3, waiting for transfers between devices, exchange(): return (part, lax.ppermute(part, 'dp', swap))  162 us
    dot_general x10, matrix products, dot(): lax.dot_general(left, right, (dims, ((), ())), preferred_element_type=jnp...  81.8 us
    all_gather x1, waiting for transfers between devices, local(): all_x = lax.all_gather(tokens, 'expert', axis=0, tiled=False)  79.2 us
    reduce_scatter x2, waiting for transfers between devices, send_home(): return lax.psum_scatter(parts, 'expert', scatter_dimension=0, tiled=True)  67.5 us
    all_gather x1, waiting for transfers between devices, local(): all_c = lax.all_gather(later, 'expert', axis=0, tiled=False)  28.5 us
    dot_general x4, matrix products, pick(): lax.dot_general(onehot, values, (((2,), (1,)), ((0,), (0,))), preferred_e...  21.9 us
    all_gather x1, blocking collectives, local(): small = lax.all_gather(small, 'expert', axis=0, tiled=False)  20 us
  transfers between devices with their start and end apart: 8, of which 6 were waited for; matrix products, arithmetic and copies ran while one was open for 21% of the time, Pallas kernels for 0%

profile of v2, /device:TPU:0, one launch (start us, length us, event | category | flops | bytes accessed | tf_op | source)
XLA Modules:
  0.0 504.2 jit_solution(17733725109698933709)
XLA Ops:
  7.2 0.0 all-gather.6.cloned.1.call-start
  7.2 0.7 all-gather.6.cloned.1.call-update
  7.9 0.0 all-gather.8.cloned.1.call-start
  7.9 79.2 %all-gather.6.cloned.1.call-done = bf16[2048,2048]{1,0:T(8,128)(2,1)} async-done(((bf16[128,2048]{1,0:T(8,128)(2,1)}), bf16[2048,2048]{1,0:T(8,128)(2,1)}) %all-gather.6.cloned.1.call-update) | async-done | bytes 8388624 | tf_op jit(solution)/shard_map/all_gather | solution.py:30
  87.2 0.0 all-gather.8.cloned.1.call-update
  87.2 0.0 reduce-scatter.3.cloned.1.call-start
  87.3 0.7 bitcast_convert_fusion
  88.0 0.7 pad_maximum_fusion
  88.6 20.0 %all-gather = f32[256,128]{1,0:T(8,128)S(1)} all-gather(f32[16,128]{1,0:T(8,128)S(1)} %pad_maximum_fusion), channel_id=2, replica_groups=mesh['dp'=2,'expert'=16] {'expert'}, dimensions={0}, use_global_device_ids=true | all-gather | bytes 139264 | tf_op jit(solution)/shard_map/all_gather | solution.py:29
  108.7 1.3 compare_reduce_fusion
  110.7 0.1 and_select_fusion
  110.8 5.3 %convolution_convert_fusion.4 = bf16[16,96,2048]{2,1,0:T(8,128)(2,1)S(1)} fusion(bf16[16,128,2048]{2,1,0:T(8,128)(2,1)} %bitcast.62, s32[16,128]{1,0:T(8,128)S(1)} %and_select_fusion), kind=kOutput, calls=%fused_computation.15 | convolution fusion | flops 808648704 | bytes 14688256 | tf_op jit(solution)/shard_map/dot_general | solution.py:12
  116.2 0.0 copy-start.8
  116.2 7.4 %fusion.15 = bf16[1536,1024]{1,0:T(8,128)(2,1)S(1)} fusion(bf16[1536,2048]{1,0:T(8,128)(2,1)S(1)} %bitcast.63, bf16[1,2048,1024]{2,1,0:T(8,128)(2,1)S(1)} %copy-done.10), kind=kOutput, calls=%fused_computation.30 | convolution fusion | flops 6444023808 | bytes 13631488 | tf_op jit(solution)/shard_map/dot_general | solution.py:8
  123.6 8.0 %fusion.12 = bf16[1536,1024]{1,0:T(8,128)(2,1)} fusion(bf16[1536,2048]{1,0:T(8,128)(2,1)S(1)} %bitcast.64, bf16[1,2048,1024]{2,1,0:T(8,128)(2,1)S(1)} %copy-done.8), kind=kOutput, calls=%fused_computation.29 | convolution fusion | flops 6444023808 | bytes 13631488 | tf_op jit(solution)/shard_map/dot_general | solution.py:8
  131.6 1.5 collective-permute-start
  133.1 0.6 collective-permute-start.1
  133.6 0.4 select_reduce_fusion.1
  134.0 0.1 mul.46
  134.1 28.5 %all-gather.8.cloned.1.call-done = bf16[2048,2048]{1,0:T(8,128)(2,1)} async-done(((bf16[128,2048]{1,0:T(8,128)(2,1)}), bf16[2048,2048]{1,0:T(8,128)(2,1)}) %all-gather.8.cloned.1.call-update) | async-done | bytes 8388624 | tf_op jit(solution)/shard_map/all_gather | solution.py:32
  162.5 5.3 %convolution_convert_fusion.3 = bf16[16,96,2048]{2,1,0:T(8,128)(2,1)S(1)} fusion(bf16[16,128,2048]{2,1,0:T(8,128)(2,1)} %bitcast.61, s32[16,128]{1,0:T(8,128)S(1)} %and_select_fusion), kind=kOutput, calls=%fused_computation.14 | convolution fusion | flops 808648704 | bytes 14688256 | tf_op jit(solution)/shard_map/dot_general | solution.py:12
  167.9 8.3 %fusion.18 = bf16[1536,1024]{1,0:T(8,128)(2,1)} fusion(bf16[1536,2048]{1,0:T(8,128)(2,1)S(1)} %bitcast.69, bf16[1,1024,2048]{2,1,0:T(8,128)(2,1)S(1)} %copy-done.7), kind=kOutput, calls=%fused_computation.31 | convolution fusion | flops 6444023808 | bytes 13631488 | tf_op jit(solution)/shard_map/dot_general | solution.py:8
  176.1 26.8 %collective-permute-done = bf16[1536,1024]{1,0:T(8,128)(2,1)} collective-permute-done((bf16[1536,1024]{1,0:T(8,128)(2,1)}, bf16[1536,1024]{1,0:T(8,128)(2,1)}, u32[]{:S(2)}, u32[]{:S(2)}) %collective-permute-start) | collective-permute-done | bytes 3145760 | tf_op jit(solution)/shard_map/ppermute | solution.py:58
  202.9 66.8 %collective-permute-done.1 = bf16[1536,1024]{1,0:T(8,128)(2,1)} collective-permute-done((bf16[1536,1024]{1,0:T(8,128)(2,1)S(1)}, bf16[1536,1024]{1,0:T(8,128)(2,1)}, u32[]{:S(2)}, u32[]{:S(2)}) %collective-permute-start.1) | collective-permute-done | bytes 3145760 | tf_op jit(solution)/shard_map/ppermute | solution.py:58
  269.7 6.5 %multiply_convert_fusion.2 = bf16[1536,1024]{1,0:T(8,128)(2,1)S(1)} fusion(bf16[1536,1024]{1,0:T(8,128)(2,1)} %collective-permute-done.1, bf16[1536,1024]{1,0:T(8,128)(2,1)S(1)} %fusion.15, bf16[1536,1024]{1,0:T(8,128)(2,1)} %collective-permute-done, bf16[1536,1024]{1,0:T(8,128)(2,1)} %fusion.12, f32[1536]{0:T(1024)S(1)} %mul.46), kind=kLoop, calls=%fused_computation.10 | loop fusion | flops 20447232 | bytes 15734784 | tf_op jit(solution)/shard_map/convert_element_type | solution.py:85
  276.2 0.0 copy-start.2
  276.2 7.1 %convolution_convert_fusion = bf16[1536,2048]{1,0:T(8,128)(2,1)S(1)} fusion(bf16[1536,1024]{1,0:T(8,128)(2,1)S(1)} %multiply_convert_fusion.2, bf16[1,1024,2048]{2,1,0:T(8,128)(2,1)S(1)} %copy-done.7), kind=kOutput, calls=%fused_computation.1 | convolution fusion | flops 6445596672 | bytes 13631488 | tf_op jit(solution)/shard_map/dot_general | solution.py:8
  283.4 5.6 %convolution_convert_fusion.2 = bf16[16,128,2048]{2,1,0:T(8,128)(2,1)} fusion(bf16[16,96,2048]{2,1,0:T(8,128)(2,1)S(1)} %bitcast.72, s32[16,128]{1,0:T(8,128)S(1)} %and_select_fusion), kind=kOutput, calls=%fused_computation.13 | convolution fusion | flops 809697280 | bytes 14688256 | tf_op jit(solution)/shard_map/dot_general | solution.py:12
  288.9 0.0 reduce-scatter.3.cloned.1.call-update
  289.0 0.0 reduce-scatter.5.cloned.1.call-start
  289.0 0.0 copy-start.9
  289.0 1.5 collective-permute-start.2
  290.6 68.2 %collective-permute-done.2 = bf16[1536,1024]{1,0:T(8,128)(2,1)S(1)} collective-permute-done((bf16[1536,1024]{1,0:T(8,128)(2,1)}, bf16[1536,1024]{1,0:T(8,128)(2,1)S(1)}, u32[]{:S(2)}, u32[]{:S(2)}) %collective-permute-start.2) | collective-permute-done | bytes 3145760 | tf_op jit(solution)/shard_map/ppermute | solution.py:58
  358.8 9.4 %multiply_reduce_fusion = (f32[1536]{0:T(1024)S(1)}, bf16[1536,1024]{1,0:T(8,128)(2,1)S(1)}, bf16[1536,1024]{1,0:T(8,128)(2,1)S(1)}) fusion(bf16[1536,1024]{1,0:T(8,128)(2,1)S(1)} %collective-permute-done.2, bf16[1536,1024]{1,0:T(8,128)(2,1)} %fusion.18, bf16[1536,1024]{1,0:T(8,128)(2,1)} %collective-permute-done.1, bf16[1536,1024]{1,0:T(8,128)(2,1)S(1)} %fusion.15, ...), kind=kLoop, calls=%fused_computation.2 | loop fusion | flops 40892928 | bytes 25178112 | tf_op jit(solution)/shard_map/reduce_sum | solution.py:107
  368.2 0.0 copy-start.5
  368.2 0.0 copy-start.11
  368.2 9.1 %fusion.8 = f32[1536,2048]{1,0:T(8,128)} fusion(bf16[1536,1024]{1,0:T(8,128)(2,1)S(1)} %get-tuple-element.33, bf16[1,2048,1024]{2,1,0:T(8,128)(2,1)S(1)} %copy-done.9), kind=kOutput, calls=%fused_computation.22 | convolution fusion | flops 6442450944 | bytes 19922944 | tf_op jit(solution)/shard_map/dot_general | solution.py:8
  377.3 9.8 %add_convert_fusion = bf16[1536,2048]{1,0:T(8,128)(2,1)S(1)} fusion(f32[1536,2048]{1,0:T(8,128)} %fusion.8, bf16[1536,1024]{1,0:T(8,128)(2,1)S(1)} %get-tuple-element.34, bf16[1,2048,1024]{2,1,0:T(8,128)(2,1)S(1)} %copy-done.11), kind=kOutput, calls=%fused_computation | convolution fusion | flops 6448742400 | bytes 26214400 | tf_op jit(solution)/shard_map/dot_general | solution.py:8
  387.1 5.6 %convolution_convert_fusion.1 = bf16[16,128,2048]{2,1,0:T(8,128)(2,1)} fusion(bf16[16,96,2048]{2,1,0:T(8,128)(2,1)S(1)} %bitcast.71, s32[16,128]{1,0:T(8,128)S(1)} %and_select_fusion), kind=kOutput, calls=%fused_computation.12 | convolution fusion | flops 809697280 | bytes 14688256 | tf_op jit(solution)/shard_map/dot_general | solution.py:12
  392.8 0.0 reduce-scatter.5.cloned.1.call-update
  392.8 11.6 %convert_bitcast_fusion = bf16[1,1024,2048]{2,1,0:T(8,128)(2,1)} fusion(bf16[1536,1024]{1,0:T(8,128)(2,1)} %copy-done.2, bf16[1536,2048]{1,0:T(8,128)(2,1)} %bitcast.70), kind=kOutput, calls=%fused_computation.26 | convolution fusion | flops 6444548096 | bytes 13631488 | tf_op jit(solution)/shard_map/dot_general | solution.py:8
  404.4 0.1 broadcast_in_dim.71
  404.4 0.9 select_reduce_fusion
  405.3 3.5 all-to-all-start
  408.8 12.0 %convert_bitcast_fusion.2 = bf16[1,2048,1024]{2,1,0:T(8,128)(2,1)} fusion(bf16[1536,2048]{1,0:T(8,128)(2,1)} %bitcast.65, bf16[1536,1024]{1,0:T(8,128)(2,1)} %copy-done.5), kind=kOutput, calls=%fused_computation.28 | convolution fusion | flops 6444548096 | bytes 13631488 | tf_op jit(solution)/shard_map/dot_general | solution.py:8
  420.8 8.5 %convert_bitcast_fusion.1 = bf16[1,2048,1024]{2,1,0:T(8,128)(2,1)} fusion(bf16[1536,2048]{1,0:T(8,128)(2,1)S(1)} %bitcast.68, bf16[1536,1024]{1,0:T(8,128)(2,1)S(1)} %copy-done.4), kind=kOutput, calls=%fused_computation.27 | convolution fusion | flops 6444548096 | bytes 13631488 | tf_op jit(solution)/shard_map/dot_general | solution.py:8
  429.3 0.6 select_reduce_fusion.2
  429.9 67.5 %reduce-scatter.5.cloned.1.call-done = bf16[128,2048]{1,0:T(8,128)(2,1)} async-done(((bf16[2048,2048]{1,0:T(8,128)(2,1)}), bf16[128,2048]{1,0:T(8,128)(2,1)}) %reduce-scatter.5.cloned.1.call-update) | async-done | bytes 524304 | tf_op jit(solution)/shard_map/reduce_scatter | solution.py:91
  (28 shorter events, 0.1 us)
Async XLA Ops:
  7.2 80.0 %all-gather.6.cloned.1.call-start = ((), (), s32[]{:S(2)}) async-start(), calls=%async_computation.5 | async-start | bytes 8912896 | tf_op jit(solution)/shard_map/all_gather | solution.py:30
  7.9 154.6 %all-gather.8.cloned.1.call-start = ((), (), s32[]{:S(2)}) async-start(), calls=%async_computation.6 | async-start | bytes 8912896 | tf_op jit(solution)/shard_map/all_gather | solution.py:32
  87.2 342.7 %reduce-scatter.3.cloned.1.call-start = ((), (), s32[]{:S(2)}) async-start(), calls=%async_computation.3 | async-start | bytes 8912896 | tf_op jit(solution)/shard_map/reduce_scatter | solution.py:91
  110.8 5.4 %copy-start.10 = (bf16[1,2048,1024]{2,1,0:T(8,128)(2,1)S(1)}, bf16[1,2048,1024]{2,1,0:T(8,128)(2,1)}, u32[]{:S(2)}) copy-start(bf16[1,2048,1024]{2,1,0:T(8,128)(2,1)} %param.14) | copy-start | bytes 12582916
  116.2 7.4 %copy-start = (bf16[16,96,2048]{2,1,0:T(8,128)(2,1)}, bf16[16,96,2048]{2,1,0:T(8,128)(2,1)S(1)}, u32[]{:S(2)}) copy-start(bf16[16,96,2048]{2,1,0:T(8,128)(2,1)S(1)} %convolution_convert_fusion.4) | copy-start | bytes 18874372
  116.2 7.4 %copy-start.8 = (bf16[1,2048,1024]{2,1,0:T(8,128)(2,1)S(1)}, bf16[1,2048,1024]{2,1,0:T(8,128)(2,1)}, u32[]{:S(2)}) copy-start(bf16[1,2048,1024]{2,1,0:T(8,128)(2,1)} %param.13) | copy-start | bytes 12582916
  131.6 71.3 %collective-permute-start = (bf16[1536,1024]{1,0:T(8,128)(2,1)}, bf16[1536,1024]{1,0:T(8,128)(2,1)}, u32[]{:S(2)}, u32[]{:S(2)}) collective-permute-start(bf16[1536,1024]{1,0:T(8,128)(2,1)} %fusion.12), channel_id=1, source_target_pairs={{0,16},{16,0},{1,17},{17,1},{2,18},{18,2},{3,19},{19,3},{4,20},{20... | collective-permute-start | bytes 9437192 | tf_op jit(solution)/shard_map/ppermute | solution.py:58
  133.1 136.6 %collective-permute-start.1 = (bf16[1536,1024]{1,0:T(8,128)(2,1)S(1)}, bf16[1536,1024]{1,0:T(8,128)(2,1)}, u32[]{:S(2)}, u32[]{:S(2)}) collective-permute-start(bf16[1536,1024]{1,0:T(8,128)(2,1)S(1)} %fusion.15), channel_id=1, source_target_pairs={{0,16},{16,0},{1,17},{17,1},{2,18},{18,2},{3,19},{19,3},{4,20},{20... | collective-permute-start | bytes 9437192 | tf_op jit(solution)/shard_map/ppermute | solution.py:58
  162.5 5.3 %copy-start.7 = (bf16[1,1024,2048]{2,1,0:T(8,128)(2,1)S(1)}, bf16[1,1024,2048]{2,1,0:T(8,128)(2,1)}, u32[]{:S(2)}) copy-start(bf16[1,1024,2048]{2,1,0:T(8,128)(2,1)} %param.15) | copy-start | bytes 12582916
  167.8 8.3 %copy-start.1 = (bf16[16,96,2048]{2,1,0:T(8,128)(2,1)}, bf16[16,96,2048]{2,1,0:T(8,128)(2,1)S(1)}, u32[]{:S(2)}) copy-start(bf16[16,96,2048]{2,1,0:T(8,128)(2,1)S(1)} %convolution_convert_fusion.3) | copy-start | bytes 18874372
  276.2 7.2 %copy-start.2 = (bf16[1536,1024]{1,0:T(8,128)(2,1)}, bf16[1536,1024]{1,0:T(8,128)(2,1)S(1)}, u32[]{:S(2)}) copy-start(bf16[1536,1024]{1,0:T(8,128)(2,1)S(1)} %multiply_convert_fusion.2) | copy-start | bytes 9437188
  289.0 208.4 %reduce-scatter.5.cloned.1.call-start = ((), (), s32[]{:S(2)}) async-start(), calls=%async_computation.4 | async-start | bytes 8912896 | tf_op jit(solution)/shard_map/reduce_scatter | solution.py:91
  289.0 79.2 %copy-start.9 = (bf16[1,2048,1024]{2,1,0:T(8,128)(2,1)S(1)}, bf16[1,2048,1024]{2,1,0:T(8,128)(2,1)}, u32[]{:S(2)}) copy-start(bf16[1,2048,1024]{2,1,0:T(8,128)(2,1)} %param.13) | copy-start | bytes 12582916
  289.0 69.7 %collective-permute-start.2 = (bf16[1536,1024]{1,0:T(8,128)(2,1)}, bf16[1536,1024]{1,0:T(8,128)(2,1)S(1)}, u32[]{:S(2)}, u32[]{:S(2)}) collective-permute-start(bf16[1536,1024]{1,0:T(8,128)(2,1)} %fusion.18), channel_id=1, source_target_pairs={{0,16},{16,0},{1,17},{17,1},{2,18},{18,2},{3,19},{19,3},{4,20},{20... | collective-permute-start | bytes 9437192 | tf_op jit(solution)/shard_map/ppermute | solution.py:58
  368.2 9.1 %copy-start.5 = (bf16[1536,1024]{1,0:T(8,128)(2,1)}, bf16[1536,1024]{1,0:T(8,128)(2,1)S(1)}, u32[]{:S(2)}) copy-start(bf16[1536,1024]{1,0:T(8,128)(2,1)S(1)} %get-tuple-element.33) | copy-start | bytes 9437188
  368.2 9.1 %copy-start.3 = (bf16[1536,1024]{1,0:T(8,128)(2,1)}, bf16[1536,1024]{1,0:T(8,128)(2,1)S(1)}, u32[]{:S(2)}) copy-start(bf16[1536,1024]{1,0:T(8,128)(2,1)S(1)} %get-tuple-element.34) | copy-start | bytes 9437188
  368.2 9.1 %copy-start.11 = (bf16[1,2048,1024]{2,1,0:T(8,128)(2,1)S(1)}, bf16[1,2048,1024]{2,1,0:T(8,128)(2,1)}, u32[]{:S(2)}) copy-start(bf16[1,2048,1024]{2,1,0:T(8,128)(2,1)} %param.14) | copy-start | bytes 12582916
  392.8 28.0 %slice-start = ((s8[6291456]{0:T(1024)(128)(4,1)}), s8[2097152]{0:T(1024)(128)(4,1)S(1)}, s32[]{:S(2)}) async-start(s8[6291456]{0:T(1024)(128)(4,1)} %bitcast.66), calls=%async_computation.7 | async-start | bytes 4194304
  405.3 24.0 %all-to-all-start = ((f32[16,1,128]{2,1,0:T(1,128)}), f32[16,1,128]{2,1,0:T(1,128)S(1)}, u32[]{:S(2)}, u32[]{:S(2)}) async-start(f32[16,1,128]{2,1,0:T(1,128)} %bitcast.14), calls=%async_computation.2 | async-start | bytes 16384 | tf_op jit(solution)/shard_map/all_to_all | solution.py:113
  408.8 12.0 %slice-start.1 = ((s8[6291456]{0:T(1024)(128)(4,1)}), s8[4194304]{0:T(1024)(128)(4,1)S(1)}, s32[]{:S(2)}) async-start(s8[6291456]{0:T(1024)(128)(4,1)} %bitcast.66), calls=%async_computation.8 | async-start | bytes 8388608
  408.8 12.0 %copy-start.4 = (bf16[1536,1024]{1,0:T(8,128)(2,1)S(1)}, bf16[1536,1024]{1,0:T(8,128)(2,1)}, u32[]{:S(2)}) copy-start(bf16[1536,1024]{1,0:T(8,128)(2,1)} %copy-done.3) | copy-start | bytes 9437188
  420.8 8.5 %copy-start.6 = (s32[128,8]{0,1:T(8,128)S(1)}, s32[128,8]{0,1:T(8,128)}, u32[]{:S(2)}) copy-start(s32[128,8]{0,1:T(8,128)} %param.9) | copy-start | bytes 12292
Sparse Core Ops, SparseCore 0:
  10.1 77.0 all-gather.5
  89.3 73.1 all-gather.7
  289.1 100.6 reduce-scatter.2
  394.3 103.0 reduce-scatter.4
